TPU v7x, 256 devices: a whole 4x4x8 slice. The times are simulated.
256 devices in a mesh: tok: 64 (over z, x, core), grp: 4 (over y).
Axes of the slice: x: 4, y: 4, z: 8, core: 2. Of those that a mesh axis runs over, the one named last changes fastest.
Arguments:
- queries: bfloat16 [4, 8192, 3072], P('grp', 'tok'), may hold values from -20 to 20, as said below
- keys: bfloat16 [4, 8192, 3072], P('grp', 'tok'), may hold values from -20 to 20, as said below
- values: bfloat16 [4, 8192, 3072], P('grp', 'tok'), may hold values from -10 to 10, as said below
- next_latent: bfloat16 [4, 8192, 3072], P('grp', 'tok'), may hold values from -20 to 20, as said below
- clip_blocks: int32 [4, 16], P('grp'), may hold values from 1 to 8, 64 in all within a row
- valid_counts: int32 [4, 64], P('grp'), may hold values from 32 to 128
- group_ids: int32 [4, 16], P('grp'), may hold values from 0 to 3
- rewards: float32 [4, 16], P('grp'), may hold values from -6 to 6
Outputs:
- velocity: bfloat16 [4, 8192, 3072], P('grp', 'tok')
- loss: float32 [], replicated
Inputs may be any that keep to these rules, and one draw needn't show every extreme that they name: queries drawn within the range. keys drawn within the range. values drawn within the range. `next_latent`: next latents drawn within the range.
All inputs are finite; a program needn't handle non-finite values.
Results may differ from a plain program's by a relative error of at most 0.0034.
Values may be sent and summed in bfloat16 or wider, within the bound.
A program may use at most 128 MiB of HBM per device.

v0:
```python
import functools
import math

import jax
import jax.numpy as jnp
from jax import lax
from jax.sharding import Mesh
from jax.sharding import PartitionSpec as P

D = 3072
HEADS = 24
HEAD = 128
BLK = 128
MAXB = 8
GROUPS = 4
TOK = ("tok_0", "tok_1", "tok_2")
TOK_GRP = ("tok_0", "tok_1", "tok_2", "grp")


masked_score = -1e30


def passed_along(value, axis, steps):
    count = lax.axis_size(axis)
    first, last = (max(0, -steps), min(count, count - steps))
    return lax.ppermute(value, axis, [(source, source + steps) for source in range(first, last)])


def by_axis(shard, axes):
    return functools.reduce(lax.psum, axes, shard)


def block_clips(clip_row, total_blocks):
    ends = jnp.cumsum(clip_row)
    positions = jnp.arange(total_blocks, dtype=jnp.int32)
    return jnp.sum((ends[None, :] <= positions[:, None]).astype(jnp.int32), axis=1)


def advantages(reward_row, group_row):
    member = (group_row[:, None] == jnp.arange(GROUPS, dtype=jnp.int32)[None, :]).astype(
        jnp.float32
    )
    totals = jnp.sum(member * reward_row[:, None], axis=0)
    counts = jnp.sum(member, axis=0)
    means = totals / jnp.maximum(counts, 1.0)
    return reward_row - jnp.sum(member * means[None, :], axis=1)


def clip_tokens(block_clip, valid_row, clips):
    member = (block_clip[:, None] == jnp.arange(clips, dtype=jnp.int32)[None, :]).astype(
        jnp.float32
    )
    return jnp.sum(member * valid_row.astype(jnp.float32)[:, None], axis=0)


def attend(query_block, key_rows, value_rows, allowed):
    width = query_block.shape[0]
    count = key_rows.shape[0]
    query_heads = query_block.reshape(width, HEADS, HEAD)
    key_heads = key_rows.reshape(count, HEADS, HEAD)
    value_heads = value_rows.reshape(count, HEADS, HEAD)
    scores = jnp.einsum(
        "qhd,khd->hqk", query_heads, key_heads, preferred_element_type=jnp.float32
    ) * (1.0 / math.sqrt(HEAD))
    scores = jnp.where(allowed[None, None, :], scores, masked_score)
    top = jnp.max(scores, axis=-1, keepdims=True)
    expo = jnp.exp(scores - top)
    probs = (expo / jnp.sum(expo, axis=-1, keepdims=True)).astype(jnp.bfloat16)
    mixed = jnp.einsum("hqk,khd->qhd", probs, value_heads, preferred_element_type=jnp.float32)
    return mixed.reshape(width, HEADS * HEAD)


def on_device(queries, keys, values, next_latent, clip_blocks, valid_counts, group_ids, rewards):
    query_rows = queries[0]
    rows = query_rows.shape[0]
    blocks_dev = rows // BLK
    devices = lax.axis_size(TOK)
    own_index = lax.axis_index(TOK)
    valid_row = valid_counts[0]
    total_blocks = valid_row.shape[0]
    block_clip = block_clips(clip_blocks[0], total_blocks)
    reach = (MAXB + blocks_dev - 2) // blocks_dev
    packed = jnp.stack([keys[0], values[0]])
    pieces = [(0, packed)]
    upward = packed
    downward = packed
    for distance in range(1, reach + 1):
        upward = passed_along(upward, TOK, 1)
        downward = passed_along(downward, TOK, -1)
        pieces.append((distance, upward))
        pieces.append((-distance, downward))
    slots = jnp.arange(BLK, dtype=jnp.int32)
    key_list = []
    value_list = []
    clip_list = []
    live_list = []
    for offset, piece in pieces:
        source = own_index - offset
        block_ids = source * blocks_dev + jnp.arange(blocks_dev, dtype=jnp.int32)
        inside = (source >= 0) & (source < devices)
        safe_ids = jnp.clip(block_ids, 0, total_blocks - 1)
        clips_here = jnp.where(inside, jnp.take(block_clip, safe_ids), -1)
        counts_here = jnp.where(inside, jnp.take(valid_row, safe_ids), 0)
        key_list.append(piece[0])
        value_list.append(piece[1])
        clip_list.append(jnp.repeat(clips_here, BLK, total_repeat_length=blocks_dev * BLK))
        live_list.append((slots[None, :] < counts_here[:, None]).reshape(-1))
    key_all = jnp.concatenate(key_list, axis=0)
    value_all = jnp.concatenate(value_list, axis=0)
    key_clip = jnp.concatenate(clip_list, axis=0)
    key_live = jnp.concatenate(live_list, axis=0)
    own_ids = own_index * blocks_dev + jnp.arange(blocks_dev, dtype=jnp.int32)
    own_clip = jnp.take(block_clip, own_ids[0])
    allowed = (key_clip == own_clip) & key_live
    mixed = attend(query_rows, key_all, value_all, allowed)
    live = slots < jnp.take(valid_row, own_ids[0])
    outputs = jnp.where(live[:, None], mixed, 0.0).astype(jnp.bfloat16)
    diff = next_latent[0].astype(jnp.float32) - outputs.astype(jnp.float32)
    token_err = jnp.sum(diff * diff, axis=-1).reshape(blocks_dev, BLK)
    own_valid = jnp.take(valid_row, own_ids)
    block_err = jnp.sum(
        token_err * (slots[None, :] < own_valid[:, None]).astype(jnp.float32), axis=1
    )
    adv = advantages(rewards[0], group_ids[0])
    tokens_of = clip_tokens(block_clip, valid_row, clip_blocks.shape[1])
    own_clips = jnp.take(block_clip, own_ids)
    terms = jnp.take(adv, own_clips) * block_err / (2.0 * D * jnp.take(tokens_of, own_clips))
    total = by_axis(jnp.sum(terms), TOK_GRP)
    return (outputs[None], total)


def solution(mesh):
    finer = Mesh(
        mesh.devices.reshape(8, 4, 2, mesh.shape["grp"]), ("tok_0", "tok_1", "tok_2", "grp")
    )
    placed = (
        P("grp", TOK, None),
        P("grp", TOK, None),
        P("grp", TOK, None),
        P("grp", TOK, None),
        P("grp", None),
        P("grp", None),
        P("grp", None),
        P("grp", None),
    )
    return jax.shard_map(
        on_device,
        mesh=finer,
        in_specs=placed,
        out_specs=(P("grp", TOK, None), P()),
        check_vma=False,
    )
```

profile of v0, /device:TPU:1, one launch (start us, length us, event | category | flops | bytes accessed | tf_op | source)
XLA Modules:
  0.0 288.1 jit_solution(6922108246525088534)
XLA Ops:
  0.6 1.5 copy.54
  2.1 1.5 copy.55
  4.9 4.5 %collective-permute-start = (bf16[2,128,3072]{1,2,0:T(8,128)(2,1)}, bf16[2,128,3072]{1,2,0:T(8,128)(2,1)}, u32[]{:S(2)}, u32[]{:S(2)}) collective-permute-start(bf16[2,128,3072]{1,2,0:T(8,128)(2,1)} %pad_maximum_fusion), channel_id=1, source_target_pairs={{0,4},{4,8},{8,12},{12,16},{16,20},{20,24},{24,28},{28,32},{32,36}... | collective-permute-start | bytes 4718600 | tf_op jit(solution)/shard_map/ppermute | solution.py:26
  9.4 3.1 %collective-permute-start.1 = (bf16[2,128,3072]{1,2,0:T(8,128)(2,1)}, bf16[2,128,3072]{1,2,0:T(8,128)(2,1)}, u32[]{:S(2)}, u32[]{:S(2)}) collective-permute-start(bf16[2,128,3072]{1,2,0:T(8,128)(2,1)} %pad_maximum_fusion), channel_id=1, source_target_pairs={{4,0},{8,4},{12,8},{16,12},{20,16},{24,20},{28,24},{32,28},{36,32}... | collective-permute-start | bytes 4718600 | tf_op jit(solution)/shard_map/ppermute | solution.py:26
  13.4 2.0 constant_dynamic-slice_fusion
  40.4 2.2 copy.79
  51.8 2.4 collective-permute-start.2
  54.2 1.5 fusion.53
  55.7 3.1 %collective-permute-start.3 = (bf16[2,128,3072]{1,2,0:T(8,128)(2,1)}, bf16[2,128,3072]{1,2,0:T(8,128)(2,1)}, u32[]{:S(2)}, u32[]{:S(2)}) collective-permute-start(bf16[2,128,3072]{1,2,0:T(8,128)(2,1)} %collective-permute-done.1), channel_id=1, source_target_pairs={{4,0},{8,4},{12,8},{16,12},{20,16},{24,20},{28,24},{32,28},{36,32}... | collective-permute-start | bytes 4718600 | tf_op jit(solution)/shard_map/ppermute | solution.py:26
  58.8 2.4 fusion.52
  61.5 1.5 copy.61
  67.2 4.7 %collective-permute-done.2 = bf16[2,128,3072]{1,2,0:T(8,128)(2,1)} collective-permute-done((bf16[2,128,3072]{1,2,0:T(8,128)(2,1)}, bf16[2,128,3072]{1,2,0:T(8,128)(2,1)}, u32[]{:S(2)}, u32[]{:S(2)}) %collective-permute-start.2) | collective-permute-done | bytes 1572896 | tf_op jit(solution)/shard_map/ppermute | solution.py:26
  71.9 4.4 %collective-permute-start.4 = (bf16[2,128,3072]{1,2,0:T(8,128)(2,1)}, bf16[2,128,3072]{1,2,0:T(8,128)(2,1)}, u32[]{:S(2)}, u32[]{:S(2)}) collective-permute-start(bf16[2,128,3072]{1,2,0:T(8,128)(2,1)} %collective-permute-done.2), channel_id=1, source_target_pairs={{0,4},{4,8},{8,12},{12,16},{16,20},{20,24},{24,28},{28,32},{32,36}... | collective-permute-start | bytes 4718600 | tf_op jit(solution)/shard_map/ppermute | solution.py:26
  77.8 1.9 collective-permute-start.5
  79.7 2.4 fusion.50
  82.4 1.5 copy.63
  88.1 5.8 %collective-permute-done.4 = bf16[2,128,3072]{1,2,0:T(8,128)(2,1)} collective-permute-done((bf16[2,128,3072]{1,2,0:T(8,128)(2,1)}, bf16[2,128,3072]{1,2,0:T(8,128)(2,1)}, u32[]{:S(2)}, u32[]{:S(2)}) %collective-permute-start.4) | collective-permute-done | bytes 1572896 | tf_op jit(solution)/shard_map/ppermute | solution.py:26
  93.9 4.4 %collective-permute-start.6 = (bf16[2,128,3072]{1,2,0:T(8,128)(2,1)}, bf16[2,128,3072]{1,2,0:T(8,128)(2,1)}, u32[]{:S(2)}, u32[]{:S(2)}) collective-permute-start(bf16[2,128,3072]{1,2,0:T(8,128)(2,1)} %collective-permute-done.4), channel_id=1, source_target_pairs={{0,4},{4,8},{8,12},{12,16},{16,20},{20,24},{24,28},{28,32},{32,36}... | collective-permute-start | bytes 4718600 | tf_op jit(solution)/shard_map/ppermute | solution.py:26
  98.3 1.5 fusion.49
  99.8 1.9 collective-permute-start.7
  101.7 2.4 fusion.48
  104.5 1.5 copy.65
  110.1 5.8 %collective-permute-done.6 = bf16[2,128,3072]{1,2,0:T(8,128)(2,1)} collective-permute-done((bf16[2,128,3072]{1,2,0:T(8,128)(2,1)}, bf16[2,128,3072]{1,2,0:T(8,128)(2,1)}, u32[]{:S(2)}, u32[]{:S(2)}) %collective-permute-start.6) | collective-permute-done | bytes 1572896 | tf_op jit(solution)/shard_map/ppermute | solution.py:26
  116.0 4.4 %collective-permute-start.8 = (bf16[2,128,3072]{1,2,0:T(8,128)(2,1)}, bf16[2,128,3072]{1,2,0:T(8,128)(2,1)}, u32[]{:S(2)}, u32[]{:S(2)}) collective-permute-start(bf16[2,128,3072]{1,2,0:T(8,128)(2,1)} %collective-permute-done.6), channel_id=1, source_target_pairs={{0,4},{4,8},{8,12},{12,16},{16,20},{20,24},{24,28},{28,32},{32,36}... | collective-permute-start | bytes 4718600 | tf_op jit(solution)/shard_map/ppermute | solution.py:26
  121.8 2.1 collective-permute-start.9
  123.9 2.4 fusion.46
  126.7 1.5 copy.67
  132.3 5.7 %collective-permute-done.8 = bf16[2,128,3072]{1,2,0:T(8,128)(2,1)} collective-permute-done((bf16[2,128,3072]{1,2,0:T(8,128)(2,1)}, bf16[2,128,3072]{1,2,0:T(8,128)(2,1)}, u32[]{:S(2)}, u32[]{:S(2)}) %collective-permute-start.8) | collective-permute-done | bytes 1572896 | tf_op jit(solution)/shard_map/ppermute | solution.py:26
  138.0 4.4 %collective-permute-start.10 = (bf16[2,128,3072]{1,2,0:T(8,128)(2,1)}, bf16[2,128,3072]{1,2,0:T(8,128)(2,1)}, u32[]{:S(2)}, u32[]{:S(2)}) collective-permute-start(bf16[2,128,3072]{1,2,0:T(8,128)(2,1)} %collective-permute-done.8), channel_id=1, source_target_pairs={{0,4},{4,8},{8,12},{12,16},{16,20},{20,24},{24,28},{28,32},{32,36}... | collective-permute-start | bytes 4718600 | tf_op jit(solution)/shard_map/ppermute | solution.py:26
  143.9 1.9 collective-permute-start.11
  145.8 2.4 fusion.44
  148.5 1.5 copy.69
  154.2 5.8 %collective-permute-done.10 = bf16[2,128,3072]{1,2,0:T(8,128)(2,1)} collective-permute-done((bf16[2,128,3072]{1,2,0:T(8,128)(2,1)}, bf16[2,128,3072]{1,2,0:T(8,128)(2,1)}, u32[]{:S(2)}, u32[]{:S(2)}) %collective-permute-start.10) | collective-permute-done | bytes 1572896 | tf_op jit(solution)/shard_map/ppermute | solution.py:26
  160.0 4.4 %collective-permute-start.12 = (bf16[2,128,3072]{1,2,0:T(8,128)(2,1)}, bf16[2,128,3072]{1,2,0:T(8,128)(2,1)}, u32[]{:S(2)}, u32[]{:S(2)}) collective-permute-start(bf16[2,128,3072]{1,2,0:T(8,128)(2,1)} %collective-permute-done.10), channel_id=1, source_target_pairs={{0,4},{4,8},{8,12},{12,16},{16,20},{20,24},{24,28},{28,32},{32,36}... | collective-permute-start | bytes 4718600 | tf_op jit(solution)/shard_map/ppermute | solution.py:26
  164.4 1.5 fusion.43
  165.9 1.9 collective-permute-start.13
  167.8 2.4 fusion.42
  170.6 1.5 copy.71
  176.4 5.7 %collective-permute-done.12 = bf16[2,128,3072]{1,2,0:T(8,128)(2,1)} collective-permute-done((bf16[2,128,3072]{1,2,0:T(8,128)(2,1)}, bf16[2,128,3072]{1,2,0:T(8,128)(2,1)}, u32[]{:S(2)}, u32[]{:S(2)}) %collective-permute-start.12) | collective-permute-done | bytes 1572896 | tf_op jit(solution)/shard_map/ppermute | solution.py:26
  183.9 4.0 %collective-permute-done.13 = bf16[2,128,3072]{1,2,0:T(8,128)(2,1)} collective-permute-done((bf16[2,128,3072]{1,2,0:T(8,128)(2,1)}, bf16[2,128,3072]{1,2,0:T(8,128)(2,1)}, u32[]{:S(2)}, u32[]{:S(2)}) %collective-permute-start.13) | collective-permute-done | bytes 1572896 | tf_op jit(solution)/shard_map/ppermute | solution.py:26
  188.0 2.4 fusion.40
  190.3 1.5 copy.73
  196.0 12.8 %fusion.55 = f32[24,128]{1,0:T(8,128)S(1)} fusion(pred[1920]{0:T(1024)(128)(4,1)S(1)} %compare_and_fusion, bf16[1920,24,128]{2,0,1:T(8,128)(2,1)} %constant_dynamic-update-slice_fusion.16, bf16[128,24,128]{2,1,0:T(8,128)(2,1)} %bitcast.190), kind=kOutput, calls=%fused_computation.134 | convolution fusion | flops 1533544320 | bytes 12597120 | tf_op jit(solution)/shard_map/sub | solution.py:67
  208.8 15.5 %fusion.8 = bf16[24,128,128]{2,1,0:T(8,128)(2,1)S(1)} fusion(bf16[1920,24,128]{0,2,1:T(8,128)(2,1)} %constant_dynamic-update-slice_fusion, f32[24,128]{1,0:T(8,128)S(1)} %fusion.55, pred[1920]{0:T(1024)(128)(4,1)S(1)} %compare_and_fusion, bf16[1920,24,128]{2,0,1:T(8,128)(2,1)} %constant_dynamic-update-slice_fusion.16, bf16[128,24,128]{2,1,0:T(8,128)(2,1)S(1)} %bitcast.191), kind=kOutput, calls=%fused_computation.10 | convolution fusion | flops 3049395200 | bytes 25180032 | tf_op jit(solution)/shard_map/hqk,khd->qhd/dot_general | solution.py:69
  226.3 23.3 %psum.28 = f32[]{:T(128)} all-reduce(f32[]{:T(128)} %bitcast.124), channel_id=1, replica_groups=mesh['tok_0'=8,'tok_1'=4,'tok_2'=2,'grp'=4] {'tok_0'}, use_global_device_ids=true, to_apply=%region_10.12 | all-reduce | flops 1 | bytes 8 | tf_op jit(solution)/shard_map/psum | solution.py:30
  249.7 24.6 %psum.29 = f32[]{:T(128)} all-reduce(f32[]{:T(128)} %psum.28), channel_id=1, replica_groups=mesh['tok_0'=8,'tok_1'=4,'tok_2'=2,'grp'=4] {'tok_1'}, use_global_device_ids=true, to_apply=%region_11.13 | all-reduce | flops 1 | bytes 8 | tf_op jit(solution)/shard_map/psum | solution.py:30
  274.5 3.1 %psum.30 = f32[]{:T(128)} all-reduce(f32[]{:T(128)} %psum.29), channel_id=1, replica_groups=mesh['tok_0'=8,'tok_1'=4,'tok_2'=2,'grp'=4] {'tok_2'}, use_global_device_ids=true, to_apply=%region_12.14 | all-reduce | flops 1 | bytes 8 | tf_op jit(solution)/shard_map/psum | solution.py:30
  278.7 9.3 %psum.31 = f32[]{:T(128)} all-reduce(f32[]{:T(128)} %psum.30), channel_id=1, replica_groups=mesh['tok_0'=8,'tok_1'=4,'tok_2'=2,'grp'=4] {'grp'}, use_global_device_ids=true, to_apply=%region_13.15 | all-reduce | flops 1 | bytes 8 | tf_op jit(solution)/shard_map/psum | solution.py:30
  (121 shorter events, 53.7 us)
Async XLA Ops:
  4.9 46.8 %collective-permute-start = (bf16[2,128,3072]{1,2,0:T(8,128)(2,1)}, bf16[2,128,3072]{1,2,0:T(8,128)(2,1)}, u32[]{:S(2)}, u32[]{:S(2)}) collective-permute-start(bf16[2,128,3072]{1,2,0:T(8,128)(2,1)} %pad_maximum_fusion), channel_id=1, source_target_pairs={{0,4},{4,8},{8,12},{12,16},{16,20},{20,24},{24,28},{28,32},{32,36}... | collective-permute-start | bytes 4718600 | tf_op jit(solution)/shard_map/ppermute | solution.py:26
  9.4 46.3 %collective-permute-start.1 = (bf16[2,128,3072]{1,2,0:T(8,128)(2,1)}, bf16[2,128,3072]{1,2,0:T(8,128)(2,1)}, u32[]{:S(2)}, u32[]{:S(2)}) collective-permute-start(bf16[2,128,3072]{1,2,0:T(8,128)(2,1)} %pad_maximum_fusion), channel_id=1, source_target_pairs={{4,0},{8,4},{12,8},{16,12},{20,16},{24,20},{28,24},{32,28},{36,32}... | collective-permute-start | bytes 4718600 | tf_op jit(solution)/shard_map/ppermute | solution.py:26
  51.8 20.1 %collective-permute-start.2 = (bf16[2,128,3072]{1,2,0:T(8,128)(2,1)}, bf16[2,128,3072]{1,2,0:T(8,128)(2,1)}, u32[]{:S(2)}, u32[]{:S(2)}) collective-permute-start(bf16[2,128,3072]{1,2,0:T(8,128)(2,1)} %collective-permute-done), channel_id=1, source_target_pairs={{0,4},{4,8},{8,12},{12,16},{16,20},{20,24},{24,28},{28,32},{32,36}... | collective-permute-start | bytes 4718600 | tf_op jit(solution)/shard_map/ppermute | solution.py:26
  55.7 22.1 %collective-permute-start.3 = (bf16[2,128,3072]{1,2,0:T(8,128)(2,1)}, bf16[2,128,3072]{1,2,0:T(8,128)(2,1)}, u32[]{:S(2)}, u32[]{:S(2)}) collective-permute-start(bf16[2,128,3072]{1,2,0:T(8,128)(2,1)} %collective-permute-done.1), channel_id=1, source_target_pairs={{4,0},{8,4},{12,8},{16,12},{20,16},{24,20},{28,24},{32,28},{36,32}... | collective-permute-start | bytes 4718600 | tf_op jit(solution)/shard_map/ppermute | solution.py:26
  71.9 22.0 %collective-permute-start.4 = (bf16[2,128,3072]{1,2,0:T(8,128)(2,1)}, bf16[2,128,3072]{1,2,0:T(8,128)(2,1)}, u32[]{:S(2)}, u32[]{:S(2)}) collective-permute-start(bf16[2,128,3072]{1,2,0:T(8,128)(2,1)} %collective-permute-done.2), channel_id=1, source_target_pairs={{0,4},{4,8},{8,12},{12,16},{16,20},{20,24},{24,28},{28,32},{32,36}... | collective-permute-start | bytes 4718600 | tf_op jit(solution)/shard_map/ppermute | solution.py:26
  77.8 22.0 %collective-permute-start.5 = (bf16[2,128,3072]{1,2,0:T(8,128)(2,1)}, bf16[2,128,3072]{1,2,0:T(8,128)(2,1)}, u32[]{:S(2)}, u32[]{:S(2)}) collective-permute-start(bf16[2,128,3072]{1,2,0:T(8,128)(2,1)} %collective-permute-done.3), channel_id=1, source_target_pairs={{4,0},{8,4},{12,8},{16,12},{20,16},{24,20},{28,24},{32,28},{36,32}... | collective-permute-start | bytes 4718600 | tf_op jit(solution)/shard_map/ppermute | solution.py:26
  93.9 22.0 %collective-permute-start.6 = (bf16[2,128,3072]{1,2,0:T(8,128)(2,1)}, bf16[2,128,3072]{1,2,0:T(8,128)(2,1)}, u32[]{:S(2)}, u32[]{:S(2)}) collective-permute-start(bf16[2,128,3072]{1,2,0:T(8,128)(2,1)} %collective-permute-done.4), channel_id=1, source_target_pairs={{0,4},{4,8},{8,12},{12,16},{16,20},{20,24},{24,28},{28,32},{32,36}... | collective-permute-start | bytes 4718600 | tf_op jit(solution)/shard_map/ppermute | solution.py:26
  99.8 22.0 %collective-permute-start.7 = (bf16[2,128,3072]{1,2,0:T(8,128)(2,1)}, bf16[2,128,3072]{1,2,0:T(8,128)(2,1)}, u32[]{:S(2)}, u32[]{:S(2)}) collective-permute-start(bf16[2,128,3072]{1,2,0:T(8,128)(2,1)} %collective-permute-done.5), channel_id=1, source_target_pairs={{4,0},{8,4},{12,8},{16,12},{20,16},{24,20},{28,24},{32,28},{36,32}... | collective-permute-start | bytes 4718600 | tf_op jit(solution)/shard_map/ppermute | solution.py:26
  116.0 22.0 %collective-permute-start.8 = (bf16[2,128,3072]{1,2,0:T(8,128)(2,1)}, bf16[2,128,3072]{1,2,0:T(8,128)(2,1)}, u32[]{:S(2)}, u32[]{:S(2)}) collective-permute-start(bf16[2,128,3072]{1,2,0:T(8,128)(2,1)} %collective-permute-done.6), channel_id=1, source_target_pairs={{0,4},{4,8},{8,12},{12,16},{16,20},{20,24},{24,28},{28,32},{32,36}... | collective-permute-start | bytes 4718600 | tf_op jit(solution)/shard_map/ppermute | solution.py:26
  121.8 22.0 %collective-permute-start.9 = (bf16[2,128,3072]{1,2,0:T(8,128)(2,1)}, bf16[2,128,3072]{1,2,0:T(8,128)(2,1)}, u32[]{:S(2)}, u32[]{:S(2)}) collective-permute-start(bf16[2,128,3072]{1,2,0:T(8,128)(2,1)} %collective-permute-done.7), channel_id=1, source_target_pairs={{4,0},{8,4},{12,8},{16,12},{20,16},{24,20},{28,24},{32,28},{36,32}... | collective-permute-start | bytes 4718600 | tf_op jit(solution)/shard_map/ppermute | solution.py:26
  138.0 22.0 %collective-permute-start.10 = (bf16[2,128,3072]{1,2,0:T(8,128)(2,1)}, bf16[2,128,3072]{1,2,0:T(8,128)(2,1)}, u32[]{:S(2)}, u32[]{:S(2)}) collective-permute-start(bf16[2,128,3072]{1,2,0:T(8,128)(2,1)} %collective-permute-done.8), channel_id=1, source_target_pairs={{0,4},{4,8},{8,12},{12,16},{16,20},{20,24},{24,28},{28,32},{32,36}... | collective-permute-start | bytes 4718600 | tf_op jit(solution)/shard_map/ppermute | solution.py:26
  143.9 22.0 %collective-permute-start.11 = (bf16[2,128,3072]{1,2,0:T(8,128)(2,1)}, bf16[2,128,3072]{1,2,0:T(8,128)(2,1)}, u32[]{:S(2)}, u32[]{:S(2)}) collective-permute-start(bf16[2,128,3072]{1,2,0:T(8,128)(2,1)} %collective-permute-done.9), channel_id=1, source_target_pairs={{4,0},{8,4},{12,8},{16,12},{20,16},{24,20},{28,24},{32,28},{36,32}... | collective-permute-start | bytes 4718600 | tf_op jit(solution)/shard_map/ppermute | solution.py:26
  160.0 22.0 %collective-permute-start.12 = (bf16[2,128,3072]{1,2,0:T(8,128)(2,1)}, bf16[2,128,3072]{1,2,0:T(8,128)(2,1)}, u32[]{:S(2)}, u32[]{:S(2)}) collective-permute-start(bf16[2,128,3072]{1,2,0:T(8,128)(2,1)} %collective-permute-done.10), channel_id=1, source_target_pairs={{0,4},{4,8},{8,12},{12,16},{16,20},{20,24},{24,28},{28,32},{32,36}... | collective-permute-start | bytes 4718600 | tf_op jit(solution)/shard_map/ppermute | solution.py:26
  165.9 22.0 %collective-permute-start.13 = (bf16[2,128,3072]{1,2,0:T(8,128)(2,1)}, bf16[2,128,3072]{1,2,0:T(8,128)(2,1)}, u32[]{:S(2)}, u32[]{:S(2)}) collective-permute-start(bf16[2,128,3072]{1,2,0:T(8,128)(2,1)} %collective-permute-done.11), channel_id=1, source_target_pairs={{4,0},{8,4},{12,8},{16,12},{20,16},{24,20},{28,24},{32,28},{36,32}... | collective-permute-start | bytes 4718600 | tf_op jit(solution)/shard_map/ppermute | solution.py:26
  196.0 12.8 %copy-start = (bf16[16,8,24,128]{3,2,1,0:T(8,128)(2,1)S(1)}, bf16[16,8,24,128]{3,2,1,0:T(8,128)(2,1)}, u32[]{:S(2)}) copy-start(bf16[16,8,24,128]{3,2,1,0:T(8,128)(2,1)} %copy.79) | copy-start | bytes 2359300
  208.8 15.8 %copy-start.1 = (bf16[1,128,3072]{2,1,0:T(8,128)(2,1)S(1)}, bf16[1,128,3072]{2,1,0:T(8,128)(2,1)}, u32[]{:S(2)}) copy-start(bf16[1,128,3072]{2,1,0:T(8,128)(2,1)} %param.73) | copy-start | bytes 2359300
where the time goes:
time: 291 us; the launch traced here: 288 us
  local copies, waits for them, and re-layouts  85.5 us (29%)
  blocking collectives  60.3 us (21%)
  starting transfers between devices  44.7 us (15%)
  waiting for transfers between devices  37.6 us (13%)
  matrix products  28.3 us (10%)
  between operations  24.8 us (9%)
  other arithmetic  6.79 us (2%)
    psum x4, blocking collectives, by_axis(): return functools.reduce(lax.psum, axes, shard)  60.3 us
    ppermute x14, starting transfers between devices, passed_along(): lax.ppermute(value, axis, [(source, source + steps) for source in range(f...  44.7 us
    ppermute x14, waiting for transfers between devices, passed_along(): lax.ppermute(value, axis, [(source, source + steps) for source in range(f...  37.6 us
    unnamed x63, local copies, waits for them, and re-layouts  37.5 us
    slice x14, local copies, waits for them, and re-layouts, on_device(): key_list.append(piece[0])  26.8 us
    dot_general x1, matrix products, attend(): jnp.einsum('hqk,khd->qhd', probs, value_heads, preferred_element_type=jnp...  15.5 us
    concatenate x16, local copies, waits for them, and re-layouts, on_device(): key_all = jnp.concatenate(key_list, axis=0)  14.6 us
    sub x1, matrix products, attend(): expo = jnp.exp(scores - top)  12.8 us
  transfers between devices with their start and end apart: 14, of which 7 were waited for; matrix products, arithmetic and copies ran while one was open for 27% of the time, Pallas kernels for 0%

commit v1 on v0

v1 whole, which is shorter than its diff:
```python
import functools
import math

import jax
import jax.numpy as jnp
from jax import lax
from jax.experimental import pallas as pl
from jax.experimental.pallas import tpu as pltpu
from jax.sharding import Mesh
from jax.sharding import PartitionSpec as P

D = 3072
HEADS = 24
HEAD = 128
BLK = 128
MAXB = 8
ROW = 8
SHARE = HEADS // ROW
SPAN = MAXB * BLK
MASKED = -1e30
TILE = (8, 128)
MESH = pl.DeviceIdType.MESH


def rows_at(block):
    return pl.ds(pl.multiple_of(block * BLK, BLK), BLK)


def tables(sizes, clip_ref, valid_ref, group_ref, reward_ref, table_ref, weight_ref):
    nz, _ = sizes
    total_blocks = nz * ROW
    clips = clip_ref.shape[1]
    z, x, c = (lax.axis_index(a) for a in ("z", "x", "c"))
    own_block = z * ROW + x * 2 + c

    def clip_of(block):
        begin = start = count = own = jnp.int32(0)
        for i in range(clips):
            size = clip_ref[0, i]
            inside = (block >= begin) & (block < begin + size)
            start = jnp.where(inside, begin, start)
            count = jnp.where(inside, size, count)
            own = jnp.where(inside, i, own)
            begin = begin + size
        return start, count, own

    def note(i, carry):
        start, count, _ = clip_of(z * ROW + i)
        table_ref[0, i] = jnp.clip(start - (z * ROW - ROW), 0, 2 * ROW)
        table_ref[0, ROW + i] = valid_ref[0, z * ROW + i]
        for j in range(MAXB):
            live = valid_ref[0, jnp.minimum(start + j, total_blocks - 1)]
            table_ref[0, 2 * ROW + i * MAXB + j] = jnp.where(j < count, live, 0)
        return carry
    lax.fori_loop(0, ROW, note, 0)

    start, count, own = clip_of(own_block)
    group = group_ref[0, own]
    total, number = jnp.float32(0), jnp.float32(0)
    for i in range(clips):
        same = group_ref[0, i] == group
        total = total + jnp.where(same, reward_ref[0, i], 0.0)
        number = number + jnp.where(same, 1.0, 0.0)
    tokens = jnp.int32(0)
    for j in range(MAXB):
        live = valid_ref[0, jnp.minimum(start + j, total_blocks - 1)]
        tokens = tokens + jnp.where(j < count, live, 0)
    mean = jnp.full(TILE, total) / jnp.full(TILE, jnp.maximum(number, 1.0))
    adv = jnp.full(TILE, reward_ref[0, own]) - mean
    weight_ref[...] = adv / jnp.full(TILE, (2.0 * D) * tokens.astype(jnp.float32))


def kernel(sizes, q_hbm, k_hbm, v_hbm, next_hbm, table_ref, weight_ref,
           out_hbm, loss_ref, kb0, kb1, kb2, vb0, vb1, vb2, qb0, qb1, qb2, ob0, ob1, ob2,
           probs, got, nxt, red_x, red_y, red_z,
           xs, xr, us, ur, ds_, dr, os_, or_, misc, rs, rr):
    nz, ng = sizes
    z, x, c, g = (lax.axis_index(a) for a in ("z", "x", "c", "grp"))
    me = x * 2 + c
    keys, vals, qrys, outs = (kb0, kb1, kb2), (vb0, vb1, vb2), (qb0, qb1, qb2), (ob0, ob1, ob2)

    def row_dev(r):
        return {"x": r // 2, "c": lax.rem(r, 2)}

    def z_dev(dz):
        return {"z": lax.rem(z + dz, nz)}

    def g_dev(dg):
        return {"grp": lax.rem(g + dg, ng)}

    def source(kind):
        return (k_hbm, v_hbm, q_hbm)[kind // SHARE]

    def landing(kind, s):
        h = kind % SHARE
        if kind < 2 * SHARE:
            return (keys, vals)[kind // SHARE][h].at[ROW + s]
        return qrys[h].at[rows_at(s), :]

    def columns(r, h):
        return pl.ds(pl.multiple_of((r * SHARE + h) * HEAD, HEAD), HEAD)

    def share_copy(kind, d, s):
        r = lax.rem(me + d, ROW)
        return pltpu.make_async_remote_copy(
            src_ref=source(kind).at[0, :, columns(r, kind % SHARE)],
            dst_ref=landing(kind, s),
            send_sem=xs.at[kind, d], recv_sem=xr.at[kind, d],
            device_id=row_dev(r), device_id_type=MESH)

    def own_copy(kind):
        return pltpu.make_async_copy(
            source(kind).at[0, :, columns(me, kind % SHARE)], landing(kind, me), xr.at[kind, 0])

    def send_share(kind):
        own_copy(kind).start()

        def body(d, carry):
            share_copy(kind, d, me).start()
            return carry
        lax.fori_loop(1, ROW, body, 0)

    def sender(d):
        return lax.rem(me + ROW - d, ROW)

    def halo_copy(kind, s, d, up):
        buf = (keys, vals)[kind // SHARE][kind % SHARE]
        return pltpu.make_async_remote_copy(
            src_ref=buf.at[ROW + s],
            dst_ref=buf.at[s if up else 2 * ROW + s],
            send_sem=(us if up else ds_).at[kind, d], recv_sem=(ur if up else dr).at[kind, d],
            device_id=z_dev(1 if up else nz - 1), device_id_type=MESH)

    def for_halo(kind, s, d, act):
        @pl.when(s != 0)
        def _():
            act(halo_copy(kind, s, d, True))

        @pl.when(s != ROW - 1)
        def _():
            act(halo_copy(kind, s, d, False))

    def forward(kind):
        own_copy(kind).wait()
        for_halo(kind, me, 0, lambda copy: copy.start())

        def body(d, carry):
            s = sender(d)
            share_copy(kind, d, s).wait_recv()
            for_halo(kind, s, d, lambda copy: copy.start())
            return carry
        lax.fori_loop(1, ROW, body, 0)

    def wait_halo(kind):
        def body(d, carry):
            for_halo(kind, sender(d), d, lambda copy: copy.wait_recv())
            return carry
        lax.fori_loop(0, ROW, body, 0)

    def wait_queries(h):
        kind = 2 * SHARE + h
        own_copy(kind).wait()

        def body(d, carry):
            share_copy(kind, d, sender(d)).wait_recv()
            return carry
        lax.fori_loop(1, ROW, body, 0)

    barrier = pltpu.get_barrier_semaphore()
    partners = ([row_dev(lax.rem(me + d, ROW)) for d in range(1, ROW)]
                + [z_dev(d) for d in range(1, nz)] + [g_dev(d) for d in range(1, ng)])
    for device in partners:
        pl.semaphore_signal(barrier, inc=1, device_id=device, device_id_type=MESH)
    pl.semaphore_wait(barrier, len(partners))

    for kind in (0, 3, 1, 4, 6, 2, 5, 7, 8):
        send_share(kind)
    latent = pltpu.make_async_copy(next_hbm.at[0], nxt, misc.at[0])
    latent.start()

    lanes = lax.broadcasted_iota(jnp.int32, (1, BLK), 1)
    slots = lax.broadcasted_iota(jnp.int32, (BLK, HEAD), 0)

    def window(buf, i):
        first = table_ref[0, i]
        return jnp.concatenate([buf[first + j] for j in range(MAXB)], axis=0)

    def score(h):
        def body(i, carry):
            query = qrys[h][rows_at(i), :]
            key = window(keys[h], i)
            scores = lax.dot_general(query, key, (((1,), (1,)), ((), ())),
                                     preferred_element_type=jnp.float32)
            bias = []
            for j in range(MAXB):
                live = table_ref[0, 2 * ROW + i * MAXB + j]
                bias.append(jnp.where(lanes < live, 0.0, MASKED))
            scores = scores * (1.0 / math.sqrt(HEAD)) + jnp.concatenate(bias, axis=1)
            top = jnp.max(scores, axis=-1, keepdims=True)
            expo = jnp.exp(scores - top)
            inverse = 1.0 / jnp.sum(expo, axis=-1, keepdims=True)
            probs[i] = (expo * inverse).astype(jnp.bfloat16)
            return carry
        lax.fori_loop(0, ROW, body, 0)

    def back_copy(h, d, r):
        return pltpu.make_async_remote_copy(
            src_ref=outs[h].at[rows_at(lax.rem(me + d, ROW)), :],
            dst_ref=got.at[:, columns(r, h)],
            send_sem=os_.at[h, d], recv_sem=or_.at[h, d],
            device_id=row_dev(lax.rem(me + d, ROW)), device_id_type=MESH)

    def home_copy(h):
        return pltpu.make_async_copy(
            outs[h].at[rows_at(me), :], got.at[:, columns(me, h)], or_.at[h, 0])

    def mix(h):
        def one(i):
            value = window(vals[h], i)
            mixed = jnp.dot(probs[i], value, preferred_element_type=jnp.float32)
            live = table_ref[0, ROW + i]
            outs[h][rows_at(i), :] = jnp.where(slots < live, mixed, 0.0).astype(jnp.bfloat16)

        def body(d, carry):
            one(lax.rem(me + d, ROW))

            @pl.when(d > 1)
            def _():
                back_copy(h, d - 1, me).start()
            return carry
        lax.fori_loop(1, ROW, body, 0)
        one(me)
        back_copy(h, ROW - 1, me).start()

    own_valid = table_ref[0, ROW + me]

    def error(h, acc):
        def body(d, total):
            r = sender(d)
            diff = (nxt[:, columns(r, h)].astype(jnp.float32)
                    - got[:, columns(r, h)].astype(jnp.float32))
            diff = jnp.where(slots < own_valid, diff, 0.0)
            return total + jnp.sum((diff * diff).reshape(BLK // 8, 8, HEAD), axis=0)
        return lax.fori_loop(0, ROW, body, acc)

    def wait_back(h):
        home_copy(h).wait()

        def body(d, carry):
            back_copy(h, d, sender(d)).wait_recv()
            return carry
        lax.fori_loop(1, ROW, body, 0)

    for kind in (0, 3, 1, 4):
        forward(kind)
    wait_queries(0)
    wait_halo(0)
    score(0)
    wait_halo(3)
    mix(0)
    home_copy(0).start()
    for kind in (2, 5):
        forward(kind)
    wait_queries(1)
    wait_halo(1)
    score(1)
    wait_halo(4)
    mix(1)
    home_copy(1).start()
    wait_queries(2)
    wait_halo(2)
    score(2)
    wait_halo(5)
    mix(2)
    home_copy(2).start()
    latent.wait()
    acc = jnp.zeros(TILE, jnp.float32)
    for h in range(SHARE):
        wait_back(h)
        acc = error(h, acc)
    acc = acc * weight_ref[...]
    home = pltpu.make_async_copy(got, out_hbm.at[0], misc.at[1])
    home.start()

    def exchange(stage, buf, place, count, device):
        def copy(d, slot):
            return pltpu.make_async_remote_copy(
                src_ref=buf.at[slot], dst_ref=buf.at[slot],
                send_sem=rs.at[stage, d], recv_sem=rr.at[stage, d],
                device_id=device(d), device_id_type=MESH)
        for d in range(1, count):
            copy(d, place).start()
        for d in range(1, count):
            copy(d, lax.rem(place + count - d, count)).wait_recv()
        total = buf[0]
        for slot in range(1, count):
            total = total + buf[slot]
        for d in range(1, count):
            copy(d, place).wait_send()
        return total

    red_x[me] = acc

    def drain(d, carry):
        for kind in range(3 * SHARE):
            share_copy(kind, d, me).wait_send()
        for h in range(SHARE):
            back_copy(h, d, me).wait_send()
        return carry
    lax.fori_loop(1, ROW, drain, 0)

    def drain_halo(d, carry):
        for kind in range(2 * SHARE):
            for_halo(kind, sender(d), d, lambda copy: copy.wait_send())
        return carry
    lax.fori_loop(0, ROW, drain_halo, 0)

    acc = exchange(0, red_x, me, ROW, lambda d: row_dev(lax.rem(me + d, ROW)))
    if ng > 1:
        red_y[g] = acc
        acc = exchange(1, red_y, g, ng, g_dev)
    red_z[z] = acc
    acc = exchange(2, red_z, z, nz, z_dev)
    loss_ref[0, 0] = jnp.sum(acc)
    home.wait()


def solution(mesh):
    ng = mesh.shape["grp"]
    nz = mesh.shape["tok"] // ROW
    finer = Mesh(mesh.devices.reshape(nz, 4, 2, ng), ("z", "x", "c", "grp"))
    tok = ("z", "x", "c")
    big = P("grp", tok, None)
    small = P("grp", None)
    dma = pltpu.SemaphoreType.DMA
    wide = pltpu.VMEM((3 * ROW, BLK, HEAD), jnp.bfloat16)
    row = pltpu.VMEM((ROW * BLK, HEAD), jnp.bfloat16)
    whole = pltpu.VMEM((BLK, D), jnp.bfloat16)
    anywhere = pl.BlockSpec(memory_space=pl.ANY)
    scalars = pl.BlockSpec(memory_space=pltpu.SMEM)

    tile = pl.BlockSpec(memory_space=pltpu.VMEM)

    def on_device(queries, keys, values, latent, *rows):
        table, weight = pl.pallas_call(
            functools.partial(tables, (nz, ng)),
            out_shape=(jax.ShapeDtypeStruct((1, 128), jnp.int32),
                       jax.ShapeDtypeStruct(TILE, jnp.float32)),
            in_specs=[scalars] * 4, out_specs=(scalars, tile),
        )(*rows)
        out, loss = pl.pallas_call(
            functools.partial(kernel, (nz, ng)),
            out_shape=(jax.ShapeDtypeStruct((1, BLK, D), jnp.bfloat16),
                       jax.ShapeDtypeStruct((1, 1), jnp.float32)),
            in_specs=[anywhere] * 4 + [scalars, tile],
            out_specs=(anywhere, scalars),
            scratch_shapes=[wide] * 6 + [row] * 6 + [
                pltpu.VMEM((ROW, BLK, SPAN), jnp.bfloat16), whole, whole,
                pltpu.VMEM((ROW, 8, 128), jnp.float32), pltpu.VMEM((max(ng, 2), 8, 128), jnp.float32),
                pltpu.VMEM((nz, 8, 128), jnp.float32),
                dma((3 * SHARE, ROW)), dma((3 * SHARE, ROW)),
                dma((2 * SHARE, ROW)), dma((2 * SHARE, ROW)),
                dma((2 * SHARE, ROW)), dma((2 * SHARE, ROW)),
                dma((SHARE, ROW)), dma((SHARE, ROW)), dma((2,)),
                dma((3, 8)), dma((3, 8))],
            compiler_params=pltpu.CompilerParams(
                collective_id=0, has_side_effects=True, vmem_limit_bytes=40 << 20),
        )(queries, keys, values, latent, table, weight)
        return out, loss.reshape(())

    return jax.shard_map(
        on_device, mesh=finer, in_specs=(big,) * 4 + (small,) * 4,
        out_specs=(big, P()), check_vma=False)
```

time: 291 us -> 79.7 us (0.27)
  local copies, waits for them, and re-layouts: 85.5 us -> 6.75 us
  Pallas kernels: 0 us -> 70.3 us
  blocking collectives: 60.3 us -> 0 us
  starting transfers between devices: 44.7 us -> 0 us
  waiting for transfers between devices: 37.6 us -> 0 us
  matrix products: 28.3 us -> 0 us
  between operations: 24.8 us -> 2.35 us
  other arithmetic: 6.79 us -> 0 us
    pallas_call x0 -> x2, Pallas kernels: none -> 70.3 us  [the longest x1 68.4 us: on_device(): pl.pallas_call(functools.partial(kernel, (nz, ng)), out_shape=(jax.ShapeD...]
    psum x4 -> x0, blocking collectives: 60.3 us -> none  [by_axis(): return functools.reduce(lax.psum, axes, shard)]
    ppermute x14 -> x0, starting transfers between devices: 44.7 us -> none  [passed_along(): lax.ppermute(value, axis, [(source, source + steps) for source in range(f...]
    ppermute x14 -> x0, waiting for transfers between devices: 37.6 us -> none  [passed_along(): lax.ppermute(value, axis, [(source, source + steps) for source in range(f...]
    unnamed x63 -> x13, local copies, waits for them, and re-layouts: 37.5 us -> 6.75 us
    slice x14 -> x0, local copies, waits for them, and re-layouts: 26.8 us -> none  [on_device(): key_list.append(piece[0])]
    concatenate x19 -> x0, local copies, waits for them, and re-layouts: 15.8 us -> none  [the longest x16 14.6 us: on_device(): key_all = jnp.concatenate(key_list, axis=0)]
    dot_general x1 -> x0, matrix products: 15.5 us -> none  [attend(): jnp.einsum('hqk,khd->qhd', probs, value_heads, preferred_element_type=jnp...]
  transfers between devices with their start and end apart: 14 -> 0, of which waited for: 7 -> 0; matrix products, arithmetic and copies ran while one was open for 27% -> 0% of each run, Pallas kernels for 0% -> 0%
where the time goes in v1:
time: 79.7 us; the launch traced here: 79.4 us
  Pallas kernels  70.3 us (88%)
  local copies, waits for them, and re-layouts  6.75 us (8%)
  between operations  2.35 us (3%)
    pallas_call x1, Pallas kernels, on_device(): pl.pallas_call(functools.partial(kernel, (nz, ng)), out_shape=(jax.ShapeD...  68.4 us
    unnamed x13, local copies, waits for them, and re-layouts  6.75 us
    pallas_call x1, Pallas kernels, on_device(): pl.pallas_call(functools.partial(tables, (nz, ng)), out_shape=(jax.ShapeD...  1.83 us

profile of v1, /device:TPU:1, one launch (start us, length us, event | category | flops | bytes accessed | tf_op | source)
XLA Modules:
  0.0 79.4 jit_solution(8611376138696008769)
XLA Ops:
  0.6 1.8 %shard_map.95 = (s32[1,128]{1,0:T(1,128)}, f32[8,128]{1,0:T(8,128)}) custom-call(s32[1,16]{1,0:T(1,128)} %clip_ref.1, s32[1,64]{1,0:T(1,128)} %valid_ref.1, s32[1,16]{1,0:T(1,128)} %group_ref.1, f32[1,16]{1,0:T(1,128)} %reward_ref.1), custom_call_target="tpu_custom_call" | custom-call | tf_op jit(solution)/shard_map/pallas_call | solution.py:345
  2.5 0.0 copy-start.5
  2.5 0.6 copy-done.5
  3.1 0.0 copy-start
  3.1 1.1 %copy-done = bf16[1,128,3072]{2,1,0:T(8,128)(2,1)S(1)} copy-done((bf16[1,128,3072]{2,1,0:T(8,128)(2,1)S(1)}, bf16[1,128,3072]{2,1,0:T(8,128)(2,1)}, u32[]{:S(2)}) %copy-start) | copy-done | bytes 786456
  4.3 0.0 copy-start.1
  4.3 1.1 %copy-done.1 = bf16[1,128,3072]{2,1,0:T(8,128)(2,1)S(1)} copy-done((bf16[1,128,3072]{2,1,0:T(8,128)(2,1)S(1)}, bf16[1,128,3072]{2,1,0:T(8,128)(2,1)}, u32[]{:S(2)}) %copy-start.1) | copy-done | bytes 786456
  5.4 0.0 copy-start.2
  5.4 1.1 %copy-done.2 = bf16[1,128,3072]{2,1,0:T(8,128)(2,1)S(1)} copy-done((bf16[1,128,3072]{2,1,0:T(8,128)(2,1)S(1)}, bf16[1,128,3072]{2,1,0:T(8,128)(2,1)}, u32[]{:S(2)}) %copy-start.2) | copy-done | bytes 786456
  6.5 0.0 copy-start.3
  6.5 1.1 %copy-done.3 = bf16[1,128,3072]{2,1,0:T(8,128)(2,1)S(1)} copy-done((bf16[1,128,3072]{2,1,0:T(8,128)(2,1)S(1)}, bf16[1,128,3072]{2,1,0:T(8,128)(2,1)}, u32[]{:S(2)}) %copy-start.3) | copy-done | bytes 786456
  7.7 0.0 copy-start.4
  7.7 0.7 copy-done.4
  8.3 68.4 %shard_map.96 = (bf16[1,128,3072]{2,1,0:T(8,128)(2,1)S(1)}, f32[1,1]{1,0:T(1,128)}) custom-call(bf16[1,128,3072]{2,1,0:T(8,128)(2,1)S(1)} %copy-done, bf16[1,128,3072]{2,1,0:T(8,128)(2,1)S(1)} %copy-done.1, bf16[1,128,3072]{2,1,0:T(8,128)(2,1)S(1)} %copy-done.2, bf16[1,128,3072]{2,1,0:T(8,128)(2,1)S(1)} %copy-done.3, s32[1,128]{1,0:T(1,128)S(1)} %copy-done.5, ...), custom_call_target="tpu_custom_call" | custom-call | tf_op jit(solution)/shard_map/pallas_call | solution.py:351
  76.8 0.9 %copy.12 = bf16[1,128,3072]{2,1,0:T(8,128)(2,1)} copy(bf16[1,128,3072]{2,1,0:T(8,128)(2,1)S(1)} %get-tuple-element.12) | data formatting | bytes 1572864
Async XLA Ops:
  2.5 0.7 copy-start.5
  3.1 1.1 %copy-start = (bf16[1,128,3072]{2,1,0:T(8,128)(2,1)S(1)}, bf16[1,128,3072]{2,1,0:T(8,128)(2,1)}, u32[]{:S(2)}) copy-start(bf16[1,128,3072]{2,1,0:T(8,128)(2,1)} %q_hbm.1) | copy-start | bytes 2359300
  4.3 1.1 %copy-start.1 = (bf16[1,128,3072]{2,1,0:T(8,128)(2,1)S(1)}, bf16[1,128,3072]{2,1,0:T(8,128)(2,1)}, u32[]{:S(2)}) copy-start(bf16[1,128,3072]{2,1,0:T(8,128)(2,1)} %k_hbm.1) | copy-start | bytes 2359300
  5.4 1.1 %copy-start.2 = (bf16[1,128,3072]{2,1,0:T(8,128)(2,1)S(1)}, bf16[1,128,3072]{2,1,0:T(8,128)(2,1)}, u32[]{:S(2)}) copy-start(bf16[1,128,3072]{2,1,0:T(8,128)(2,1)} %v_hbm.1) | copy-start | bytes 2359300
  6.5 1.1 %copy-start.3 = (bf16[1,128,3072]{2,1,0:T(8,128)(2,1)S(1)}, bf16[1,128,3072]{2,1,0:T(8,128)(2,1)}, u32[]{:S(2)}) copy-start(bf16[1,128,3072]{2,1,0:T(8,128)(2,1)} %next_hbm.1) | copy-start | bytes 2359300
  7.7 0.7 copy-start.4

commit v2 on v1

v2 whole, which is shorter than its diff:
```python
import functools
import math

import jax
import jax.numpy as jnp
from jax import lax
from jax.experimental import pallas as pl
from jax.experimental.pallas import tpu as pltpu
from jax.sharding import Mesh
from jax.sharding import PartitionSpec as P

D = 3072
HEADS = 24
HEAD = 128
BLK = 128
MAXB = 8
ROW = 8
SHARE = HEADS // ROW
SPAN = MAXB * BLK
MASKED = -1e30
TILE = (8, 128)
MESH = pl.DeviceIdType.MESH


def rows_at(block):
    return pl.ds(pl.multiple_of(block * BLK, BLK), BLK)


def kernel(sizes, q_hbm, k_hbm, v_hbm, next_hbm, clip_ref, valid_ref, group_ref, reward_ref,
           out_hbm, loss_ref, kb0, kb1, kb2, vb0, vb1, vb2, qb0, qb1, qb2, ob0, ob1, ob2,
           probs, got, nxt, first_ref, live_ref, red_xy, red_z,
           xs, xr, us, ur, ds_, dr, os_, or_, misc, rs, rr):
    nz, ng = sizes
    total_blocks = nz * ROW
    clips = clip_ref.shape[1]
    z, x, c, g = (lax.axis_index(a) for a in ("z", "x", "c", "grp"))
    me = x * 2 + c
    keys, vals, qrys, outs = (kb0, kb1, kb2), (vb0, vb1, vb2), (qb0, qb1, qb2), (ob0, ob1, ob2)

    def row_dev(r):
        return {"x": r // 2, "c": lax.rem(r, 2)}

    def z_dev(dz):
        return {"z": lax.rem(z + dz, nz)}

    def g_dev(dg):
        return {"grp": lax.rem(g + dg, ng)}

    def source(kind):
        return (k_hbm, v_hbm, q_hbm)[kind // SHARE]

    def landing(kind, s):
        h = kind % SHARE
        if kind < 2 * SHARE:
            return (keys, vals)[kind // SHARE][h].at[ROW + s]
        return qrys[h].at[rows_at(s), :]

    def columns(r, h):
        return pl.ds(pl.multiple_of((r * SHARE + h) * HEAD, HEAD), HEAD)

    def share_copy(kind, d, s):
        r = lax.rem(me + d, ROW)
        return pltpu.make_async_remote_copy(
            src_ref=source(kind).at[0, :, columns(r, kind % SHARE)],
            dst_ref=landing(kind, s),
            send_sem=xs.at[kind, d], recv_sem=xr.at[kind, d],
            device_id=row_dev(r), device_id_type=MESH)

    def own_copy(kind):
        return pltpu.make_async_copy(
            source(kind).at[0, :, columns(me, kind % SHARE)], landing(kind, me), xr.at[kind, 0])

    def send_share(kind):
        own_copy(kind).start()

        def body(d, carry):
            share_copy(kind, d, me).start()
            return carry
        lax.fori_loop(1, ROW, body, 0)

    def sender(d):
        return lax.rem(me + ROW - d, ROW)

    def halo_copy(kind, s, d, up, own):
        buf = (keys, vals)[kind // SHARE][kind % SHARE]
        return pltpu.make_async_remote_copy(
            src_ref=source(kind).at[0, :, columns(me, kind % SHARE)] if own else buf.at[ROW + s],
            dst_ref=buf.at[s if up else 2 * ROW + s],
            send_sem=(us if up else ds_).at[kind, d], recv_sem=(ur if up else dr).at[kind, d],
            device_id=z_dev(1 if up else nz - 1), device_id_type=MESH)

    def for_halo(kind, s, d, act, own=False):
        @pl.when(s != 0)
        def _():
            act(halo_copy(kind, s, d, True, own))

        @pl.when(s != ROW - 1)
        def _():
            act(halo_copy(kind, s, d, False, own))

    def forward_one(kind, t):
        d = 1 + lax.rem(t + 6 * (1 - c), ROW - 1)
        s = sender(d)
        share_copy(kind, d, s).wait_recv()
        for_halo(kind, s, d, lambda copy: copy.start())

    def forward(kind):
        def body(t, carry):
            forward_one(kind, t)
            return carry
        lax.fori_loop(0, ROW - 1, body, 0)

    def wait_halo(kind):
        own_copy(kind).wait()

        def body(d, carry):
            for_halo(kind, sender(d), d, lambda copy: copy.wait_recv())
            return carry
        lax.fori_loop(0, ROW, body, 0)

    def wait_queries(h):
        kind = 2 * SHARE + h
        own_copy(kind).wait()

        def body(d, carry):
            share_copy(kind, d, sender(d)).wait_recv()
            return carry
        lax.fori_loop(1, ROW, body, 0)

    barrier = pltpu.get_barrier_semaphore()
    near, far = ROW * ng, nz

    def near_dev(p):
        r = lax.rem(me + p // ng, ROW)
        return {"x": r // 2, "c": lax.rem(r, 2), "grp": lax.rem(g + lax.rem(p, ng), ng)}

    def greet(device):
        def body(p, carry):
            pl.semaphore_signal(barrier, inc=1, device_id=device(p), device_id_type=MESH)
            return carry
        return body
    lax.fori_loop(1, far, greet(z_dev), 0)
    lax.fori_loop(1, near, greet(near_dev), 0)
    pl.semaphore_wait(barrier, near + far - 2)

    order = (0, 3, 6, 1, 4, 7, 2, 5, 8)
    for kind in order[:2]:
        send_share(kind)
    for kind in (0, 3, 1, 4, 2, 5):
        for_halo(kind, me, 0, lambda copy: copy.start(), own=True)
    for kind in order[2:]:
        send_share(kind)
    latent = pltpu.make_async_copy(next_hbm.at[0], nxt, misc.at[0])
    latent.start()

    def clip_of(block):
        def body(i, carry):
            begin, start, count, own = carry
            size = clip_ref[0, i]
            inside = (block >= begin) & (block < begin + size)
            return (begin + size, jnp.where(inside, begin, start), jnp.where(inside, size, count),
                    jnp.where(inside, i, own))
        zero = jnp.int32(0)
        _, start, count, own = lax.fori_loop(0, clips, body, (zero, zero, zero, zero))
        return start, count, own

    def note(i, carry):
        start, count, _ = clip_of(z * ROW + i)
        first_ref[i] = jnp.clip(start - (z * ROW - ROW), 0, 2 * ROW)
        for j in range(MAXB):
            live = valid_ref[0, jnp.minimum(start + j, total_blocks - 1)]
            live_ref[i * MAXB + j] = jnp.where(j < count, live, 0)
        return carry
    lax.fori_loop(0, ROW, note, 0)

    own_block = z * ROW + me
    own_start, own_count, own_clip = clip_of(own_block)
    own_group = group_ref[0, own_clip]
    own_valid = valid_ref[0, own_block]

    def member(i, carry):
        total, count = carry
        same = group_ref[0, i] == own_group
        return (total + jnp.where(same, reward_ref[0, i], 0.0), count + jnp.where(same, 1.0, 0.0))
    total, count = lax.fori_loop(0, clips, member, (jnp.float32(0), jnp.float32(0)))
    tokens = jnp.int32(0)
    for j in range(MAXB):
        live = valid_ref[0, jnp.minimum(own_start + j, total_blocks - 1)]
        tokens = tokens + jnp.where(j < own_count, live, 0)
    mean = jnp.full(TILE, total) / jnp.full(TILE, jnp.maximum(count, 1.0))
    adv = jnp.full(TILE, reward_ref[0, own_clip]) - mean
    weight = adv / jnp.full(TILE, (2.0 * D) * tokens.astype(jnp.float32))

    lanes = lax.broadcasted_iota(jnp.int32, (1, BLK), 1)
    slots = lax.broadcasted_iota(jnp.int32, (BLK, HEAD), 0)

    def window(buf, i):
        first = first_ref[i]
        return jnp.concatenate([buf[first + j] for j in range(MAXB)], axis=0)

    def score(h):
        def one(i):
            query = qrys[h][rows_at(i), :]
            key = window(keys[h], i)
            scores = lax.dot_general(query, key, (((1,), (1,)), ((), ())),
                                     preferred_element_type=jnp.float32)
            bias = []
            for j in range(MAXB):
                live = live_ref[i * MAXB + j]
                bias.append(jnp.where(lanes < live, 0.0, MASKED))
            scores = scores * (1.0 / math.sqrt(HEAD)) + jnp.concatenate(bias, axis=1)
            top = jnp.max(scores, axis=-1, keepdims=True)
            expo = jnp.exp(scores - top)
            inverse = 1.0 / jnp.sum(expo, axis=-1, keepdims=True)
            return (expo * inverse).astype(jnp.bfloat16)

        def body(n, carry):
            if h + 1 < SHARE:
                forward_one(h + 1, 2 * n)

                @pl.when(n < ROW // 2 - 1)
                def _():
                    forward_one(h + 1, 2 * n + 1)
            first, second = one(2 * n), one(2 * n + 1)
            probs[2 * n] = first
            probs[2 * n + 1] = second
            return carry
        lax.fori_loop(0, ROW // 2, body, 0)

    def back_copy(h, d, r):
        return pltpu.make_async_remote_copy(
            src_ref=outs[h].at[rows_at(lax.rem(me + d, ROW)), :],
            dst_ref=got.at[:, columns(r, h)],
            send_sem=os_.at[h, d], recv_sem=or_.at[h, d],
            device_id=row_dev(lax.rem(me + d, ROW)), device_id_type=MESH)

    def home_copy(h):
        return pltpu.make_async_copy(
            outs[h].at[rows_at(me), :], got.at[:, columns(me, h)], or_.at[h, 0])

    def mix(h):
        def one(i):
            value = window(vals[h], i)
            mixed = jnp.dot(probs[i], value, preferred_element_type=jnp.float32)
            live = valid_ref[0, z * ROW + i]
            outs[h][rows_at(i), :] = jnp.where(slots < live, mixed, 0.0).astype(jnp.bfloat16)

        def body(d, carry):
            one(lax.rem(me + d, ROW))

            @pl.when(d > 1)
            def _():
                back_copy(h, d - 1, me).start()
            if h + 1 < SHARE:
                forward_one(SHARE + h + 1, d - 1)
            return carry
        lax.fori_loop(1, ROW, body, 0)
        one(me)
        back_copy(h, ROW - 1, me).start()

    def error(h, acc):
        def body(d, total):
            r = sender(d)
            diff = (nxt[:, columns(r, h)].astype(jnp.float32)
                    - got[:, columns(r, h)].astype(jnp.float32))
            diff = jnp.where(slots < own_valid, diff, 0.0)
            return total + jnp.sum((diff * diff).reshape(BLK // 8, 8, HEAD), axis=0)
        return lax.fori_loop(0, ROW, body, acc)

    def wait_back(h):
        home_copy(h).wait()

        def body(d, carry):
            back_copy(h, d, sender(d)).wait_recv()
            return carry
        lax.fori_loop(1, ROW, body, 0)

    forward(0)
    forward(SHARE)
    for h in range(SHARE):
        wait_queries(h)
        wait_halo(h)
        score(h)
        wait_halo(SHARE + h)
        mix(h)
        home_copy(h).start()
    latent.wait()
    acc = jnp.zeros(TILE, jnp.float32)
    for h in range(SHARE):
        wait_back(h)
        acc = error(h, acc)

    def exchange(buf, stage, place, other, count, device, between):
        def copy(p, slot):
            return pltpu.make_async_remote_copy(
                src_ref=buf.at[slot], dst_ref=buf.at[slot],
                send_sem=rs.at[stage, p], recv_sem=rr.at[stage, p],
                device_id=device(p), device_id_type=MESH)

        def start(p, carry):
            copy(p, place).start()
            return carry

        def land(p, carry):
            copy(p, other(p)).wait_recv()
            return carry

        def sent(p, carry):
            copy(p, place).wait_send()
            return carry
        lax.fori_loop(1, count, start, 0)
        between()
        lax.fori_loop(1, count, land, 0)
        total = jnp.sum(buf[...], axis=0)
        return total, lambda: lax.fori_loop(1, count, sent, 0)

    def drain(d, carry):
        for kind in range(3 * SHARE):
            share_copy(kind, d, me).wait_send()
        for h in range(SHARE):
            back_copy(h, d, me).wait_send()
        return carry

    def drain_halo(d, carry):
        for kind in range(2 * SHARE):
            for_halo(kind, sender(d), d, lambda copy: copy.wait_send())
        return carry

    red_xy[me * ng + g] = jnp.sum(acc, axis=0, keepdims=True) * weight[:1]
    home = pltpu.make_async_copy(got, out_hbm.at[0], misc.at[1])
    home.start()
    acc, sent_near = exchange(
        red_xy, 0, me * ng + g,
        lambda p: lax.rem(me + ROW - p // ng, ROW) * ng + lax.rem(g + ng - lax.rem(p, ng), ng),
        near, near_dev, lambda: lax.fori_loop(1, ROW, drain, 0))
    red_z[z] = acc
    acc, sent_far = exchange(
        red_z, 1, z, lambda p: lax.rem(z + nz - p, nz), far, z_dev,
        lambda: lax.fori_loop(0, ROW, drain_halo, 0))
    loss_ref[0, 0] = jnp.sum(acc)
    sent_near()
    sent_far()
    home.wait()


def solution(mesh):
    ng = mesh.shape["grp"]
    nz = mesh.shape["tok"] // ROW
    finer = Mesh(mesh.devices.reshape(nz, 4, 2, ng), ("z", "x", "c", "grp"))
    tok = ("z", "x", "c")
    big = P("grp", tok, None)
    small = P("grp", None)
    dma = pltpu.SemaphoreType.DMA
    wide = pltpu.VMEM((3 * ROW, BLK, HEAD), jnp.bfloat16)
    row = pltpu.VMEM((ROW * BLK, HEAD), jnp.bfloat16)
    whole = pltpu.VMEM((BLK, D), jnp.bfloat16)
    anywhere = pl.BlockSpec(memory_space=pl.ANY)
    scalars = pl.BlockSpec(memory_space=pltpu.SMEM)


    def on_device(*args):
        out, loss = pl.pallas_call(
            functools.partial(kernel, (nz, ng)),
            out_shape=(jax.ShapeDtypeStruct((1, BLK, D), jnp.bfloat16),
                       jax.ShapeDtypeStruct((1, 1), jnp.float32)),
            in_specs=[anywhere] * 4 + [scalars] * 4,
            out_specs=(anywhere, scalars),
            scratch_shapes=[wide] * 6 + [row] * 6 + [
                pltpu.VMEM((ROW, BLK, SPAN), jnp.bfloat16), whole, whole,
                pltpu.SMEM((ROW,), jnp.int32), pltpu.SMEM((ROW * MAXB,), jnp.int32),
                pltpu.VMEM((ROW * ng, 1, 128), jnp.float32), pltpu.VMEM((nz, 1, 128), jnp.float32),
                dma((3 * SHARE, ROW)), dma((3 * SHARE, ROW)),
                dma((2 * SHARE, ROW)), dma((2 * SHARE, ROW)),
                dma((2 * SHARE, ROW)), dma((2 * SHARE, ROW)),
                dma((SHARE, ROW)), dma((SHARE, ROW)), dma((2,)),
                dma((2, ROW * ng)), dma((2, ROW * ng))],
            compiler_params=pltpu.CompilerParams(
                collective_id=0, has_side_effects=True),
        )(*args)
        return out, loss.reshape(())

    return jax.shard_map(
        on_device, mesh=finer, in_specs=(big,) * 4 + (small,) * 4,
        out_specs=(big, P()), check_vma=False)
```

time: 79.7 us -> 70.2 us (0.88)
  local copies, waits for them, and re-layouts: 6.75 us -> 2.06 us
  Pallas kernels: 70.3 us -> 65.7 us
    unnamed x13 -> x1, local copies, waits for them, and re-layouts: 6.75 us -> 2.06 us
    pallas_call x1, Pallas kernels: 68.4 us -> 65.7 us  [on_device(): pl.pallas_call(functools.partial(kernel, (nz, ng)), out_shape=(jax.ShapeD...]
    pallas_call x1 -> x0, Pallas kernels: 1.83 us -> none  [on_device(): pl.pallas_call(functools.partial(tables, (nz, ng)), out_shape=(jax.ShapeD...]
where the time goes in v2:
time: 70.2 us; the launch traced here: 70.1 us
  Pallas kernels  65.7 us (94%)
  between operations  2.32 us (3%)
  local copies, waits for them, and re-layouts  2.06 us (3%)
    pallas_call x1, Pallas kernels, on_device(): pl.pallas_call(functools.partial(kernel, (nz, ng)), out_shape=(jax.ShapeD...  65.7 us
    unnamed x1, local copies, waits for them, and re-layouts  2.06 us

profile of v2, /device:TPU:1, one launch (start us, length us, event | category | flops | bytes accessed | tf_op | source)
XLA Modules:
  0.0 70.1 jit_solution(8628838379509598252)
XLA Ops:
  0.6 65.7 %shard_map.95 = (bf16[1,128,3072]{2,1,0:T(8,128)(2,1)}, f32[1,1]{1,0:T(1,128)}) custom-call(bf16[1,128,3072]{2,1,0:T(8,128)(2,1)} %q_hbm.1, bf16[1,128,3072]{2,1,0:T(8,128)(2,1)} %k_hbm.1, bf16[1,128,3072]{2,1,0:T(8,128)(2,1)} %v_hbm.1, bf16[1,128,3072]{2,1,0:T(8,128)(2,1)} %next_hbm.1, s32[1,16]{1,0:T(1,128)} %clip_ref.1, s32[1,64]{1,0:T(1,128)} %valid_ref.1, ...), custom_call_target="tpu_custom_call" | custom-call | tf_op jit(solution)/shard_map/pallas_call | solution.py:362
  66.4 2.1 %copy.12 = bf16[1,128,3072]{2,1,0:T(8,128)(2,1)} copy(bf16[1,128,3072]{2,1,0:T(8,128)(2,1)} %get-tuple-element.8) | data formatting | bytes 1572864

commit v3 on v2

--- a/solution.py
+++ b/solution.py
@@ -19,6 +19,7 @@
 SPAN = MAXB * BLK
 MASKED = -1e30
 TILE = (8, 128)
+LAST = 3 * SHARE
 MESH = pl.DeviceIdType.MESH
 
 
@@ -27,9 +28,9 @@
 
 
 def kernel(sizes, q_hbm, k_hbm, v_hbm, next_hbm, clip_ref, valid_ref, group_ref, reward_ref,
-           out_hbm, loss_ref, kb0, kb1, kb2, vb0, vb1, vb2, qb0, qb1, qb2, ob0, ob1, ob2,
-           probs, got, nxt, first_ref, live_ref, red_xy, red_z,
-           xs, xr, us, ur, ds_, dr, os_, or_, misc, rs, rr):
+           out_hbm, loss_ref, kb0, kb1, kb2, vb0, vb1, vb2, qb0, qb1, qb2, ob0, ob1, ob2, nb,
+           probs, got, nxt, weights, first_ref, live_ref, red_zg, red_x,
+           xs, xr, us, ur, ds_, dr, os_, or_, misc, rs, rr, word):
     nz, ng = sizes
     total_blocks = nz * ROW
     clips = clip_ref.shape[1]
@@ -47,36 +48,42 @@
         return {"grp": lax.rem(g + dg, ng)}
 
     def source(kind):
-        return (k_hbm, v_hbm, q_hbm)[kind // SHARE]
+        return (k_hbm, v_hbm, q_hbm, next_hbm)[kind // SHARE]
 
     def landing(kind, s):
-        h = kind % SHARE
+        h = head_of(kind)
+        if kind == LAST:
+            return nb.at[rows_at(s), :]
         if kind < 2 * SHARE:
             return (keys, vals)[kind // SHARE][h].at[ROW + s]
         return qrys[h].at[rows_at(s), :]
 
+    def head_of(kind):
+        return SHARE - 1 if kind == LAST else kind % SHARE
+
     def columns(r, h):
         return pl.ds(pl.multiple_of((r * SHARE + h) * HEAD, HEAD), HEAD)
 
     def share_copy(kind, d, s):
         r = lax.rem(me + d, ROW)
         return pltpu.make_async_remote_copy(
-            src_ref=source(kind).at[0, :, columns(r, kind % SHARE)],
+            src_ref=source(kind).at[0, :, columns(r, head_of(kind))],
             dst_ref=landing(kind, s),
             send_sem=xs.at[kind, d], recv_sem=xr.at[kind, d],
             device_id=row_dev(r), device_id_type=MESH)
 
     def own_copy(kind):
         return pltpu.make_async_copy(
-            source(kind).at[0, :, columns(me, kind % SHARE)], landing(kind, me), xr.at[kind, 0])
+            source(kind).at[0, :, columns(me, head_of(kind))], landing(kind, me), xr.at[kind, 0])
+
+    def nth(t):
+        return 1 + lax.rem(t + 6 * c, ROW - 1)
 
     def send_share(kind):
-        own_copy(kind).start()
-
-        def body(d, carry):
-            share_copy(kind, d, me).start()
-            return carry
-        lax.fori_loop(1, ROW, body, 0)
+        def body(t, carry):
+            share_copy(kind, nth(t), me).start()
+            return carry
+        lax.fori_loop(1, ROW - 1, body, 0)
 
     def sender(d):
         return lax.rem(me + ROW - d, ROW)
@@ -98,8 +105,11 @@
         def _():
             act(halo_copy(kind, s, d, False, own))
 
+    def rnth(t):
+        return 1 + lax.rem(t + 6 * (1 - c), ROW - 1)
+
     def forward_one(kind, t):
-        d = 1 + lax.rem(t + 6 * (1 - c), ROW - 1)
+        d = rnth(t)
         s = sender(d)
         share_copy(kind, d, s).wait_recv()
         for_halo(kind, s, d, lambda copy: copy.start())
@@ -108,7 +118,7 @@
         def body(t, carry):
             forward_one(kind, t)
             return carry
-        lax.fori_loop(0, ROW - 1, body, 0)
+        lax.fori_loop(1, ROW - 1, body, 0)
 
     def wait_halo(kind):
         own_copy(kind).wait()
@@ -118,8 +128,7 @@
             return carry
         lax.fori_loop(0, ROW, body, 0)
 
-    def wait_queries(h):
-        kind = 2 * SHARE + h
+    def wait_share(kind):
         own_copy(kind).wait()
 
         def body(d, carry):
@@ -128,28 +137,37 @@
         lax.fori_loop(1, ROW, body, 0)
 
     barrier = pltpu.get_barrier_semaphore()
-    near, far = ROW * ng, nz
-
-    def near_dev(p):
-        r = lax.rem(me + p // ng, ROW)
-        return {"x": r // 2, "c": lax.rem(r, 2), "grp": lax.rem(g + lax.rem(p, ng), ng)}
-
-    def greet(device):
-        def body(p, carry):
-            pl.semaphore_signal(barrier, inc=1, device_id=device(p), device_id_type=MESH)
-            return carry
-        return body
-    lax.fori_loop(1, far, greet(z_dev), 0)
-    lax.fori_loop(1, near, greet(near_dev), 0)
-    pl.semaphore_wait(barrier, near + far - 2)
-
-    order = (0, 3, 6, 1, 4, 7, 2, 5, 8)
+    across = [z_dev(1), z_dev(nz - 1), g_dev(1), g_dev(ng - 1)]
+
+    def greet(d, carry):
+        pl.semaphore_signal(barrier, inc=1, device_id=row_dev(lax.rem(me + d, ROW)), device_id_type=MESH)
+        return carry
+    for device in across:
+        pl.semaphore_signal(barrier, inc=1, device_id=device, device_id_type=MESH)
+    lax.fori_loop(1, ROW, greet, 0)
+    pl.semaphore_wait(barrier, ROW - 1 + len(across))
+
+    def tell(n, devices):
+        for device in devices:
+            pl.semaphore_signal(word.at[n], inc=1, device_id=device, device_id_type=MESH)
+
+    hops = nz // 2
+    tell(0, across)
+
+    order = (0, 3, 6, 1, 4, 7, 2, 5, 8, LAST)
+    streams = (0, 3, 1, 4, 2, 5)
+    for kind in order:
+        share_copy(kind, nth(0), me).start()
     for kind in order[:2]:
         send_share(kind)
-    for kind in (0, 3, 1, 4, 2, 5):
+    for kind in streams:
         for_halo(kind, me, 0, lambda copy: copy.start(), own=True)
+    for kind in streams:
+        forward_one(kind, 0)
     for kind in order[2:]:
         send_share(kind)
+    for kind in order:
+        own_copy(kind).start()
     latent = pltpu.make_async_copy(next_hbm.at[0], nxt, misc.at[0])
     latent.start()
 
@@ -173,24 +191,24 @@
         return carry
     lax.fori_loop(0, ROW, note, 0)
 
-    own_block = z * ROW + me
-    own_start, own_count, own_clip = clip_of(own_block)
-    own_group = group_ref[0, own_clip]
-    own_valid = valid_ref[0, own_block]
-
-    def member(i, carry):
-        total, count = carry
-        same = group_ref[0, i] == own_group
-        return (total + jnp.where(same, reward_ref[0, i], 0.0), count + jnp.where(same, 1.0, 0.0))
-    total, count = lax.fori_loop(0, clips, member, (jnp.float32(0), jnp.float32(0)))
-    tokens = jnp.int32(0)
-    for j in range(MAXB):
-        live = valid_ref[0, jnp.minimum(own_start + j, total_blocks - 1)]
-        tokens = tokens + jnp.where(j < own_count, live, 0)
-    mean = jnp.full(TILE, total) / jnp.full(TILE, jnp.maximum(count, 1.0))
-    adv = jnp.full(TILE, reward_ref[0, own_clip]) - mean
-    weight = adv / jnp.full(TILE, (2.0 * D) * tokens.astype(jnp.float32))
-
+    def weigh(b, carry):
+        start, count, own = clip_of(z * ROW + b)
+        group = group_ref[0, own]
+
+        def member(i, sums):
+            total, number = sums
+            same = group_ref[0, i] == group
+            return (total + jnp.where(same, reward_ref[0, i], 0.0), number + jnp.where(same, 1.0, 0.0))
+        total, number = lax.fori_loop(0, clips, member, (jnp.float32(0), jnp.float32(0)))
+        tokens = jnp.int32(0)
+        for j in range(MAXB):
+            tokens = tokens + live_ref[b * MAXB + j]
+        mean = jnp.full(TILE, total) / jnp.full(TILE, jnp.maximum(number, 1.0))
+        adv = jnp.full(TILE, reward_ref[0, own]) - mean
+        weights[b] = adv / jnp.full(TILE, (2.0 * D) * tokens.astype(jnp.float32))
+        return carry
+
+    own_valid = valid_ref[0, z * ROW + me]
     lanes = lax.broadcasted_iota(jnp.int32, (1, BLK), 1)
     slots = lax.broadcasted_iota(jnp.int32, (BLK, HEAD), 0)
 
@@ -216,11 +234,10 @@
 
         def body(n, carry):
             if h + 1 < SHARE:
-                forward_one(h + 1, 2 * n)
-
                 @pl.when(n < ROW // 2 - 1)
                 def _():
                     forward_one(h + 1, 2 * n + 1)
+                    forward_one(h + 1, 2 * n + 2)
             first, second = one(2 * n), one(2 * n + 1)
             probs[2 * n] = first
             probs[2 * n + 1] = second
@@ -238,34 +255,49 @@
         return pltpu.make_async_copy(
             outs[h].at[rows_at(me), :], got.at[:, columns(me, h)], or_.at[h, 0])
 
-    def mix(h):
+    def squares(latent_block, velocity_block, live):
+        diff = latent_block.astype(jnp.float32) - velocity_block.astype(jnp.float32)
+        diff = jnp.where(slots < live, diff, 0.0)
+        return jnp.sum((diff * diff).reshape(BLK // 8, 8, HEAD), axis=0)
+
+    def mix(h, total):
         def one(i):
-            value = window(vals[h], i)
-            mixed = jnp.dot(probs[i], value, preferred_element_type=jnp.float32)
+            mixed = jnp.dot(probs[i], window(vals[h], i), preferred_element_type=jnp.float32)
             live = valid_ref[0, z * ROW + i]
-            outs[h][rows_at(i), :] = jnp.where(slots < live, mixed, 0.0).astype(jnp.bfloat16)
-
-        def body(d, carry):
-            one(lax.rem(me + d, ROW))
-
-            @pl.when(d > 1)
+            mixed = jnp.where(slots < live, mixed, 0.0).astype(jnp.bfloat16)
+            if h < SHARE - 1:
+                return mixed, 0.0
+            return mixed, squares(nb[rows_at(i), :], mixed, live) * weights[i]
+
+        def pair(d, e, total):
+            first, second = lax.rem(me + d, ROW), lax.rem(me + e, ROW)
+            (one_first, err_first), (one_second, err_second) = one(first), one(second)
+            outs[h][rows_at(first), :] = one_first
+            outs[h][rows_at(second), :] = one_second
+            return total + err_first + err_second
+
+        def body(n, total):
+            total = pair(2 * n + 2, 2 * n + 3, total)
+
+            @pl.when(n > 0)
             def _():
-                back_copy(h, d - 1, me).start()
+                back_copy(h, 2 * n, me).start()
+                back_copy(h, 2 * n + 1, me).start()
             if h + 1 < SHARE:
-                forward_one(SHARE + h + 1, d - 1)
-            return carry
-        lax.fori_loop(1, ROW, body, 0)
-        one(me)
-        back_copy(h, ROW - 1, me).start()
-
-    def error(h, acc):
+                forward_one(SHARE + h + 1, 2 * n + 1)
+                forward_one(SHARE + h + 1, 2 * n + 2)
+            return total
+        total = lax.fori_loop(0, ROW // 2 - 1, body, total)
+        total = pair(1, 0, total)
+        for d in (ROW - 2, ROW - 1, 1):
+            back_copy(h, d, me).start()
+        return total
+
+    def error(h):
         def body(d, total):
             r = sender(d)
-            diff = (nxt[:, columns(r, h)].astype(jnp.float32)
-                    - got[:, columns(r, h)].astype(jnp.float32))
-            diff = jnp.where(slots < own_valid, diff, 0.0)
-            return total + jnp.sum((diff * diff).reshape(BLK // 8, 8, HEAD), axis=0)
-        return lax.fori_loop(0, ROW, body, acc)
+            return total + squares(nxt[:, columns(r, h)], got[:, columns(r, h)], own_valid)
+        return lax.fori_loop(0, ROW, body, jnp.zeros(TILE, jnp.float32)) * weights[me]
 
     def wait_back(h):
         home_copy(h).wait()
@@ -276,19 +308,30 @@
         lax.fori_loop(1, ROW, body, 0)
 
     forward(0)
+    pl.semaphore_wait(word.at[0], len(across))
+    tell(1, across[:2])
     forward(SHARE)
+    for n in range(1, hops - 1):
+        pl.semaphore_wait(word.at[n], 2)
+        tell(n + 1, across[:2] if n < hops - 2 else [g_dev(d) for d in range(1, ng)])
+    acc = jnp.zeros(TILE, jnp.float32)
     for h in range(SHARE):
-        wait_queries(h)
+        wait_share(2 * SHARE + h)
+        if h == 1:
+            lax.fori_loop(0, ROW, weigh, 0)
+        if h == SHARE - 1:
+            wait_share(LAST)
         wait_halo(h)
         score(h)
         wait_halo(SHARE + h)
-        mix(h)
+        if h == SHARE - 1:
+            latent.wait()
+            for e in range(SHARE - 1):
+                wait_back(e)
+                acc = acc + error(e)
+        acc = mix(h, acc)
         home_copy(h).start()
-    latent.wait()
-    acc = jnp.zeros(TILE, jnp.float32)
-    for h in range(SHARE):
-        wait_back(h)
-        acc = error(h, acc)
+    pl.semaphore_wait(word.at[hops - 1], ng - 1)
 
     def exchange(buf, stage, place, other, count, device, between):
         def copy(p, slot):
@@ -298,7 +341,7 @@
                 device_id=device(p), device_id_type=MESH)
 
         def start(p, carry):
-            copy(p, place).start()
+            copy(1 + lax.rem(p + count // 2 - 2, count - 1), place).start()
             return carry
 
         def land(p, carry):
@@ -315,7 +358,7 @@
         return total, lambda: lax.fori_loop(1, count, sent, 0)
 
     def drain(d, carry):
-        for kind in range(3 * SHARE):
+        for kind in range(3 * SHARE + 1):
             share_copy(kind, d, me).wait_send()
         for h in range(SHARE):
             back_copy(h, d, me).wait_send()
@@ -326,20 +369,28 @@
             for_halo(kind, sender(d), d, lambda copy: copy.wait_send())
         return carry
 
-    red_xy[me * ng + g] = jnp.sum(acc, axis=0, keepdims=True) * weight[:1]
+    red_zg[z * ng + g] = jnp.sum(acc, axis=0, keepdims=True)
     home = pltpu.make_async_copy(got, out_hbm.at[0], misc.at[1])
-    home.start()
-    acc, sent_near = exchange(
-        red_xy, 0, me * ng + g,
-        lambda p: lax.rem(me + ROW - p // ng, ROW) * ng + lax.rem(g + ng - lax.rem(p, ng), ng),
-        near, near_dev, lambda: lax.fori_loop(1, ROW, drain, 0))
-    red_z[z] = acc
-    acc, sent_far = exchange(
-        red_z, 1, z, lambda p: lax.rem(z + nz - p, nz), far, z_dev,
+
+    def rest():
+        wait_back(SHARE - 1)
+        home.start()
+        lax.fori_loop(1, ROW, drain, 0)
+
+    def plane_dev(p):
+        return {"z": lax.rem(z + p // ng, nz), "grp": lax.rem(g + lax.rem(p, ng), ng)}
+
+    acc, sent_plane = exchange(
+        red_zg, 0, z * ng + g,
+        lambda p: lax.rem(z + nz - p // ng, nz) * ng + lax.rem(g + ng - lax.rem(p, ng), ng),
+        nz * ng, plane_dev, rest)
+    red_x[me] = acc
+    acc, sent_row = exchange(
+        red_x, 1, me, lambda p: lax.rem(me + ROW - p, ROW), ROW, lambda p: row_dev(lax.rem(me + p, ROW)),
         lambda: lax.fori_loop(0, ROW, drain_halo, 0))
     loss_ref[0, 0] = jnp.sum(acc)
-    sent_near()
-    sent_far()
+    sent_plane()
+    sent_row()
     home.wait()
 
 
@@ -365,15 +416,17 @@
                        jax.ShapeDtypeStruct((1, 1), jnp.float32)),
             in_specs=[anywhere] * 4 + [scalars] * 4,
             out_specs=(anywhere, scalars),
-            scratch_shapes=[wide] * 6 + [row] * 6 + [
+            scratch_shapes=[wide] * 6 + [row] * 7 + [
                 pltpu.VMEM((ROW, BLK, SPAN), jnp.bfloat16), whole, whole,
+                pltpu.VMEM((ROW, 8, 128), jnp.float32),
                 pltpu.SMEM((ROW,), jnp.int32), pltpu.SMEM((ROW * MAXB,), jnp.int32),
-                pltpu.VMEM((ROW * ng, 1, 128), jnp.float32), pltpu.VMEM((nz, 1, 128), jnp.float32),
-                dma((3 * SHARE, ROW)), dma((3 * SHARE, ROW)),
+                pltpu.VMEM((nz * ng, 1, 128), jnp.float32), pltpu.VMEM((ROW, 1, 128), jnp.float32),
+                dma((3 * SHARE + 1, ROW)), dma((3 * SHARE + 1, ROW)),
                 dma((2 * SHARE, ROW)), dma((2 * SHARE, ROW)),
                 dma((2 * SHARE, ROW)), dma((2 * SHARE, ROW)),
                 dma((SHARE, ROW)), dma((SHARE, ROW)), dma((2,)),
-                dma((2, ROW * ng)), dma((2, ROW * ng))],
+                dma((2, nz * ng)), dma((2, nz * ng)),
+                pltpu.SemaphoreType.REGULAR((nz // 2,))],
             compiler_params=pltpu.CompilerParams(
                 collective_id=0, has_side_effects=True),
         )(*args)

time: 70.2 us -> 68.1 us (0.970)
  Pallas kernels: 65.7 us -> 63.6 us
    pallas_call x1, Pallas kernels: 65.7 us -> 63.6 us  [on_device(): pl.pallas_call(functools.partial(kernel, (nz, ng)), out_shape=(jax.ShapeD...]
where the time goes in v3:
time: 68.1 us; the launch traced here: 68 us
  Pallas kernels  63.6 us (93%)
  between operations  2.32 us (3%)
  local copies, waits for them, and re-layouts  2.06 us (3%)
    pallas_call x1, Pallas kernels, on_device(): pl.pallas_call(functools.partial(kernel, (nz, ng)), out_shape=(jax.ShapeD...  63.6 us
    unnamed x1, local copies, waits for them, and re-layouts  2.06 us

profile of v3, /device:TPU:1, one launch (start us, length us, event | category | flops | bytes accessed | tf_op | source)
XLA Modules:
  0.0 68.0 jit_solution(5719738736677496075)
XLA Ops:
  0.6 63.6 %shard_map.95 = (bf16[1,128,3072]{2,1,0:T(8,128)(2,1)}, f32[1,1]{1,0:T(1,128)}) custom-call(bf16[1,128,3072]{2,1,0:T(8,128)(2,1)} %q_hbm.1, bf16[1,128,3072]{2,1,0:T(8,128)(2,1)} %k_hbm.1, bf16[1,128,3072]{2,1,0:T(8,128)(2,1)} %v_hbm.1, bf16[1,128,3072]{2,1,0:T(8,128)(2,1)} %next_hbm.1, s32[1,16]{1,0:T(1,128)} %clip_ref.1, s32[1,64]{1,0:T(1,128)} %valid_ref.1, ...), custom_call_target="tpu_custom_call" | custom-call | tf_op jit(solution)/shard_map/pallas_call | solution.py:413
  64.2 2.1 %copy.12 = bf16[1,128,3072]{2,1,0:T(8,128)(2,1)} copy(bf16[1,128,3072]{2,1,0:T(8,128)(2,1)} %get-tuple-element.8) | data formatting | bytes 1572864

commit v4 on v3

--- a/solution.py
+++ b/solution.py
@@ -30,7 +30,7 @@
 def kernel(sizes, q_hbm, k_hbm, v_hbm, next_hbm, clip_ref, valid_ref, group_ref, reward_ref,
            out_hbm, loss_ref, kb0, kb1, kb2, vb0, vb1, vb2, qb0, qb1, qb2, ob0, ob1, ob2, nb,
            probs, got, nxt, weights, first_ref, live_ref, red_zg, red_x,
-           xs, xr, us, ur, ds_, dr, os_, or_, misc, rs, rr, word):
+           xs, xr, qr, own, zs, zr, os_, or_, misc, rs, rr, word):
     nz, ng = sizes
     total_blocks = nz * ROW
     clips = clip_ref.shape[1]
@@ -69,12 +69,18 @@
         return pltpu.make_async_remote_copy(
             src_ref=source(kind).at[0, :, columns(r, head_of(kind))],
             dst_ref=landing(kind, s),
-            send_sem=xs.at[kind, d], recv_sem=xr.at[kind, d],
+            send_sem=xs.at[kind], recv_sem=xr.at[kind, d] if kind < 2 * SHARE else qr.at[kind - 2 * SHARE],
             device_id=row_dev(r), device_id_type=MESH)
+
+    def whole_share(kind):
+        part = qb0.at[pl.ds(0, (ROW - 1) * BLK), :]
+        return pltpu.make_async_remote_copy(
+            src_ref=part, dst_ref=part, send_sem=xs.at[kind], recv_sem=qr.at[max(kind - 2 * SHARE, 0)],
+            device_id=row_dev(lax.rem(me + 1, ROW)), device_id_type=MESH)
 
     def own_copy(kind):
         return pltpu.make_async_copy(
-            source(kind).at[0, :, columns(me, head_of(kind))], landing(kind, me), xr.at[kind, 0])
+            source(kind).at[0, :, columns(me, head_of(kind))], landing(kind, me), own.at[kind])
 
     def nth(t):
         return 1 + lax.rem(t + 6 * c, ROW - 1)
@@ -93,7 +99,7 @@
         return pltpu.make_async_remote_copy(
             src_ref=source(kind).at[0, :, columns(me, kind % SHARE)] if own else buf.at[ROW + s],
             dst_ref=buf.at[s if up else 2 * ROW + s],
-            send_sem=(us if up else ds_).at[kind, d], recv_sem=(ur if up else dr).at[kind, d],
+            send_sem=zs.at[kind], recv_sem=zr.at[kind, 0 if up else 1],
             device_id=z_dev(1 if up else nz - 1), device_id_type=MESH)
 
     def for_halo(kind, s, d, act, own=False):
@@ -120,21 +126,22 @@
             return carry
         lax.fori_loop(1, ROW - 1, body, 0)
 
+    def whole_halo(kind, up):
+        buf = (keys, vals)[kind // SHARE][kind % SHARE]
+        both = buf.at[pl.ds(0, 2 * (ROW - 1))]
+        side = buf.at[pl.ds(1 if up else 2 * ROW, ROW - 1)]
+        return pltpu.make_async_remote_copy(
+            src_ref=both, dst_ref=side, send_sem=zs.at[kind], recv_sem=zr.at[kind, 0 if up else 1],
+            device_id=z_dev(1 if up else nz - 1), device_id_type=MESH)
+
     def wait_halo(kind):
         own_copy(kind).wait()
-
-        def body(d, carry):
-            for_halo(kind, sender(d), d, lambda copy: copy.wait_recv())
-            return carry
-        lax.fori_loop(0, ROW, body, 0)
+        whole_halo(kind, True).wait_recv()
+        whole_halo(kind, False).wait_recv()
 
     def wait_share(kind):
         own_copy(kind).wait()
-
-        def body(d, carry):
-            share_copy(kind, d, sender(d)).wait_recv()
-            return carry
-        lax.fori_loop(1, ROW, body, 0)
+        whole_share(kind).wait_recv()
 
     barrier = pltpu.get_barrier_semaphore()
     across = [z_dev(1), z_dev(nz - 1), g_dev(1), g_dev(ng - 1)]
@@ -248,12 +255,12 @@
         return pltpu.make_async_remote_copy(
             src_ref=outs[h].at[rows_at(lax.rem(me + d, ROW)), :],
             dst_ref=got.at[:, columns(r, h)],
-            send_sem=os_.at[h, d], recv_sem=or_.at[h, d],
+            send_sem=os_.at[h], recv_sem=or_.at[h],
             device_id=row_dev(lax.rem(me + d, ROW)), device_id_type=MESH)
 
     def home_copy(h):
         return pltpu.make_async_copy(
-            outs[h].at[rows_at(me), :], got.at[:, columns(me, h)], or_.at[h, 0])
+            outs[h].at[rows_at(me), :], got.at[:, columns(me, h)], own.at[LAST + 1 + h])
 
     def squares(latent_block, velocity_block, live):
         diff = latent_block.astype(jnp.float32) - velocity_block.astype(jnp.float32)
@@ -299,13 +306,15 @@
             return total + squares(nxt[:, columns(r, h)], got[:, columns(r, h)], own_valid)
         return lax.fori_loop(0, ROW, body, jnp.zeros(TILE, jnp.float32)) * weights[me]
 
+    def whole_back(h):
+        part = outs[h].at[pl.ds(0, (ROW - 1) * BLK), :]
+        return pltpu.make_async_remote_copy(
+            src_ref=part, dst_ref=part, send_sem=os_.at[h], recv_sem=or_.at[h],
+            device_id=row_dev(lax.rem(me + 1, ROW)), device_id_type=MESH)
+
     def wait_back(h):
         home_copy(h).wait()
-
-        def body(d, carry):
-            back_copy(h, d, sender(d)).wait_recv()
-            return carry
-        lax.fori_loop(1, ROW, body, 0)
+        whole_back(h).wait_recv()
 
     forward(0)
     pl.semaphore_wait(word.at[0], len(across))
@@ -323,51 +332,40 @@
             wait_share(LAST)
         wait_halo(h)
         score(h)
-        wait_halo(SHARE + h)
         if h == SHARE - 1:
             latent.wait()
-            for e in range(SHARE - 1):
-                wait_back(e)
-                acc = acc + error(e)
+            wait_back(0)
+            acc = acc + error(0)
+        wait_halo(SHARE + h)
         acc = mix(h, acc)
         home_copy(h).start()
+    wait_back(1)
+    acc = acc + error(1)
     pl.semaphore_wait(word.at[hops - 1], ng - 1)
 
-    def exchange(buf, stage, place, other, count, device, between):
-        def copy(p, slot):
-            return pltpu.make_async_remote_copy(
-                src_ref=buf.at[slot], dst_ref=buf.at[slot],
-                send_sem=rs.at[stage, p], recv_sem=rr.at[stage, p],
-                device_id=device(p), device_id_type=MESH)
-
+    def exchange(buf, stage, place, count, device, between):
         def start(p, carry):
-            copy(1 + lax.rem(p + count // 2 - 2, count - 1), place).start()
-            return carry
-
-        def land(p, carry):
-            copy(p, other(p)).wait_recv()
-            return carry
-
-        def sent(p, carry):
-            copy(p, place).wait_send()
+            far = 1 + lax.rem(p + count // 2 - 2, count - 1)
+            pltpu.make_async_remote_copy(
+                src_ref=buf.at[place], dst_ref=buf.at[place], send_sem=rs.at[stage], recv_sem=rr.at[stage],
+                device_id=device(far), device_id_type=MESH).start()
             return carry
         lax.fori_loop(1, count, start, 0)
         between()
-        lax.fori_loop(1, count, land, 0)
+        whole = pltpu.make_async_remote_copy(
+            src_ref=buf.at[pl.ds(0, count - 1)], dst_ref=buf.at[pl.ds(0, count - 1)],
+            send_sem=rs.at[stage], recv_sem=rr.at[stage], device_id=device(1), device_id_type=MESH)
+        whole.wait_recv()
         total = jnp.sum(buf[...], axis=0)
-        return total, lambda: lax.fori_loop(1, count, sent, 0)
-
-    def drain(d, carry):
+        return total, whole.wait_send
+
+    def drain():
         for kind in range(3 * SHARE + 1):
-            share_copy(kind, d, me).wait_send()
+            whole_share(kind).wait_send()
+        for kind in range(2 * SHARE):
+            whole_halo(kind, True).wait_send()
         for h in range(SHARE):
-            back_copy(h, d, me).wait_send()
-        return carry
-
-    def drain_halo(d, carry):
-        for kind in range(2 * SHARE):
-            for_halo(kind, sender(d), d, lambda copy: copy.wait_send())
-        return carry
+            whole_back(h).wait_send()
 
     red_zg[z * ng + g] = jnp.sum(acc, axis=0, keepdims=True)
     home = pltpu.make_async_copy(got, out_hbm.at[0], misc.at[1])
@@ -375,19 +373,16 @@
     def rest():
         wait_back(SHARE - 1)
         home.start()
-        lax.fori_loop(1, ROW, drain, 0)
-
     def plane_dev(p):
         return {"z": lax.rem(z + p // ng, nz), "grp": lax.rem(g + lax.rem(p, ng), ng)}
 
     acc, sent_plane = exchange(
         red_zg, 0, z * ng + g,
-        lambda p: lax.rem(z + nz - p // ng, nz) * ng + lax.rem(g + ng - lax.rem(p, ng), ng),
         nz * ng, plane_dev, rest)
     red_x[me] = acc
     acc, sent_row = exchange(
-        red_x, 1, me, lambda p: lax.rem(me + ROW - p, ROW), ROW, lambda p: row_dev(lax.rem(me + p, ROW)),
-        lambda: lax.fori_loop(0, ROW, drain_halo, 0))
+        red_x, 1, me, ROW, lambda p: row_dev(lax.rem(me + p, ROW)),
+        drain)
     loss_ref[0, 0] = jnp.sum(acc)
     sent_plane()
     sent_row()
@@ -421,11 +416,9 @@
                 pltpu.VMEM((ROW, 8, 128), jnp.float32),
                 pltpu.SMEM((ROW,), jnp.int32), pltpu.SMEM((ROW * MAXB,), jnp.int32),
                 pltpu.VMEM((nz * ng, 1, 128), jnp.float32), pltpu.VMEM((ROW, 1, 128), jnp.float32),
-                dma((3 * SHARE + 1, ROW)), dma((3 * SHARE + 1, ROW)),
-                dma((2 * SHARE, ROW)), dma((2 * SHARE, ROW)),
-                dma((2 * SHARE, ROW)), dma((2 * SHARE, ROW)),
-                dma((SHARE, ROW)), dma((SHARE, ROW)), dma((2,)),
-                dma((2, nz * ng)), dma((2, nz * ng)),
+                dma((LAST + 1,)), dma((2 * SHARE, ROW)), dma((SHARE + 1,)), dma((LAST + 1 + SHARE,)),
+                dma((2 * SHARE,)), dma((2 * SHARE, 2)), dma((SHARE,)), dma((SHARE,)), dma((2,)),
+                dma((2,)), dma((2,)),
                 pltpu.SemaphoreType.REGULAR((nz // 2,))],
             compiler_params=pltpu.CompilerParams(
                 collective_id=0, has_side_effects=True),

time: 68.1 us -> 62.7 us (0.921)
  Pallas kernels: 63.6 us -> 58.1 us
    pallas_call x1, Pallas kernels: 63.6 us -> 58.1 us  [on_device(): pl.pallas_call(functools.partial(kernel, (nz, ng)), out_shape=(jax.ShapeD...]
where the time goes in v4:
time: 62.7 us; the launch traced here: 62.5 us
  Pallas kernels  58.1 us (93%)
  between operations  2.32 us (4%)
  local copies, waits for them, and re-layouts  2.06 us (3%)
    pallas_call x1, Pallas kernels, on_device(): pl.pallas_call(functools.partial(kernel, (nz, ng)), out_shape=(jax.ShapeD...  58.1 us
    unnamed x1, local copies, waits for them, and re-layouts  2.06 us

profile of v4, /device:TPU:1, one launch (start us, length us, event | category | flops | bytes accessed | tf_op | source)
XLA Modules:
  0.0 62.5 jit_solution(4365388757927936693)
XLA Ops:
  0.6 58.1 %shard_map.95 = (bf16[1,128,3072]{2,1,0:T(8,128)(2,1)}, f32[1,1]{1,0:T(1,128)}) custom-call(bf16[1,128,3072]{2,1,0:T(8,128)(2,1)} %q_hbm.1, bf16[1,128,3072]{2,1,0:T(8,128)(2,1)} %k_hbm.1, bf16[1,128,3072]{2,1,0:T(8,128)(2,1)} %v_hbm.1, bf16[1,128,3072]{2,1,0:T(8,128)(2,1)} %next_hbm.1, s32[1,16]{1,0:T(1,128)} %clip_ref.1, s32[1,64]{1,0:T(1,128)} %valid_ref.1, ...), custom_call_target="tpu_custom_call" | custom-call | tf_op jit(solution)/shard_map/pallas_call | solution.py:408
  58.8 2.1 %copy.12 = bf16[1,128,3072]{2,1,0:T(8,128)(2,1)} copy(bf16[1,128,3072]{2,1,0:T(8,128)(2,1)} %get-tuple-element.8) | data formatting | bytes 1572864

commit v5 on v4

--- a/solution.py
+++ b/solution.py
@@ -27,10 +27,16 @@
     return pl.ds(pl.multiple_of(block * BLK, BLK), BLK)
 
 
-def kernel(sizes, q_hbm, k_hbm, v_hbm, next_hbm, clip_ref, valid_ref, group_ref, reward_ref,
-           out_hbm, loss_ref, kb0, kb1, kb2, vb0, vb1, vb2, qb0, qb1, qb2, ob0, ob1, ob2, nb,
-           probs, got, nxt, weights, first_ref, live_ref, red_zg, red_x,
-           xs, xr, qr, own, zs, zr, os_, or_, misc, rs, rr, word):
+def kernel(sizes, q_hbm, k_hbm, v_hbm, next_hbm, *rest):
+    small_hbm, rest = rest[:4], rest[4:]
+    (out_hbm, loss_ref, kb0, kb1, kb2, vb0, vb1, vb2, qb0, qb1, qb2, ob0, ob1, ob2, nb,
+     probs, got, nxt, weights, first_ref, live_ref, red_zg, red_x,
+     xs, xr, qr, own, zs, zr, os_, or_, misc, rs, rr, word,
+     clip_ref, valid_ref, group_ref, reward_ref, small) = rest
+    rows = [pltpu.make_async_copy(a, b, small.at[n]) for n, (a, b) in enumerate(
+        zip(small_hbm, (clip_ref, valid_ref, group_ref, reward_ref)))]
+    for copy in rows:
+        copy.start()
     nz, ng = sizes
     total_blocks = nz * ROW
     clips = clip_ref.shape[1]
@@ -161,12 +167,12 @@
     hops = nz // 2
     tell(0, across)
 
-    order = (0, 3, 6, 1, 4, 7, 2, 5, 8, LAST)
+    order = (0, 3, 1, 6, 4, 2, 7, 5, 8, LAST)
     streams = (0, 3, 1, 4, 2, 5)
-    for kind in order:
+    send_share(order[0])
+    for kind in streams:
         share_copy(kind, nth(0), me).start()
-    for kind in order[:2]:
-        send_share(kind)
+    send_share(order[1])
     for kind in streams:
         for_halo(kind, me, 0, lambda copy: copy.start(), own=True)
     for kind in streams:
@@ -174,6 +180,8 @@
     for kind in order[2:]:
         send_share(kind)
     for kind in order:
+        if kind not in streams:
+            share_copy(kind, nth(0), me).start()
         own_copy(kind).start()
     latent = pltpu.make_async_copy(next_hbm.at[0], nxt, misc.at[0])
     latent.start()
@@ -188,6 +196,9 @@
         zero = jnp.int32(0)
         _, start, count, own = lax.fori_loop(0, clips, body, (zero, zero, zero, zero))
         return start, count, own
+
+    for copy in rows:
+        copy.wait()
 
     def note(i, carry):
         start, count, _ = clip_of(z * ROW + i)
@@ -223,7 +234,7 @@
         first = first_ref[i]
         return jnp.concatenate([buf[first + j] for j in range(MAXB)], axis=0)
 
-    def score(h):
+    def score(h, beside):
         def one(i):
             query = qrys[h][rows_at(i), :]
             key = window(keys[h], i)
@@ -240,11 +251,11 @@
             return (expo * inverse).astype(jnp.bfloat16)
 
         def body(n, carry):
-            if h + 1 < SHARE:
+            if beside is not None:
                 @pl.when(n < ROW // 2 - 1)
                 def _():
-                    forward_one(h + 1, 2 * n + 1)
-                    forward_one(h + 1, 2 * n + 2)
+                    forward_one(beside, 2 * n + 1)
+                    forward_one(beside, 2 * n + 2)
             first, second = one(2 * n), one(2 * n + 1)
             probs[2 * n] = first
             probs[2 * n + 1] = second
@@ -267,7 +278,7 @@
         diff = jnp.where(slots < live, diff, 0.0)
         return jnp.sum((diff * diff).reshape(BLK // 8, 8, HEAD), axis=0)
 
-    def mix(h, total):
+    def mix(h, total, beside):
         def one(i):
             mixed = jnp.dot(probs[i], window(vals[h], i), preferred_element_type=jnp.float32)
             live = valid_ref[0, z * ROW + i]
@@ -290,9 +301,9 @@
             def _():
                 back_copy(h, 2 * n, me).start()
                 back_copy(h, 2 * n + 1, me).start()
-            if h + 1 < SHARE:
-                forward_one(SHARE + h + 1, 2 * n + 1)
-                forward_one(SHARE + h + 1, 2 * n + 2)
+            if beside is not None:
+                forward_one(beside, 2 * n + 1)
+                forward_one(beside, 2 * n + 2)
             return total
         total = lax.fori_loop(0, ROW // 2 - 1, body, total)
         total = pair(1, 0, total)
@@ -325,20 +336,21 @@
         tell(n + 1, across[:2] if n < hops - 2 else [g_dev(d) for d in range(1, ng)])
     acc = jnp.zeros(TILE, jnp.float32)
     for h in range(SHARE):
+        if h == SHARE - 1:
+            lax.fori_loop(0, ROW, weigh, 0)
         wait_share(2 * SHARE + h)
-        if h == 1:
-            lax.fori_loop(0, ROW, weigh, 0)
-        if h == SHARE - 1:
-            wait_share(LAST)
         wait_halo(h)
-        score(h)
+        score(h, (1, 5, None)[h])
         if h == SHARE - 1:
             latent.wait()
             wait_back(0)
             acc = acc + error(0)
+            wait_share(LAST)
         wait_halo(SHARE + h)
-        acc = mix(h, acc)
+        acc = mix(h, acc, (4, None, None)[h])
         home_copy(h).start()
+        if h == 0:
+            forward(2)
     wait_back(1)
     acc = acc + error(1)
     pl.semaphore_wait(word.at[hops - 1], ng - 1)
@@ -409,7 +421,7 @@
             functools.partial(kernel, (nz, ng)),
             out_shape=(jax.ShapeDtypeStruct((1, BLK, D), jnp.bfloat16),
                        jax.ShapeDtypeStruct((1, 1), jnp.float32)),
-            in_specs=[anywhere] * 4 + [scalars] * 4,
+            in_specs=[anywhere] * 8,
             out_specs=(anywhere, scalars),
             scratch_shapes=[wide] * 6 + [row] * 7 + [
                 pltpu.VMEM((ROW, BLK, SPAN), jnp.bfloat16), whole, whole,
@@ -419,7 +431,8 @@
                 dma((LAST + 1,)), dma((2 * SHARE, ROW)), dma((SHARE + 1,)), dma((LAST + 1 + SHARE,)),
                 dma((2 * SHARE,)), dma((2 * SHARE, 2)), dma((SHARE,)), dma((SHARE,)), dma((2,)),
                 dma((2,)), dma((2,)),
-                pltpu.SemaphoreType.REGULAR((nz // 2,))],
+                pltpu.SemaphoreType.REGULAR((nz // 2,)),
+                *(pltpu.SMEM(a.shape, a.dtype) for a in args[4:]), dma((4,))],
             compiler_params=pltpu.CompilerParams(
                 collective_id=0, has_side_effects=True),
         )(*args)

time: 62.7 us -> 62 us (0.989)
    pallas_call x1, Pallas kernels: 58.1 us -> 57.5 us  [on_device(): pl.pallas_call(functools.partial(kernel, (nz, ng)), out_shape=(jax.ShapeD...]
where the time goes in v5:
time: 62 us; the launch traced here: 61.9 us
  Pallas kernels  57.5 us (93%)
  between operations  2.32 us (4%)
  local copies, waits for them, and re-layouts  2.06 us (3%)
    pallas_call x1, Pallas kernels, on_device(): pl.pallas_call(functools.partial(kernel, (nz, ng)), out_shape=(jax.ShapeD...  57.5 us
    unnamed x1, local copies, waits for them, and re-layouts  2.06 us

profile of v5, /device:TPU:1, one launch (start us, length us, event | category | flops | bytes accessed | tf_op | source)
XLA Modules:
  0.0 61.9 jit_solution(14796658152282967942)
XLA Ops:
  0.6 57.5 %shard_map.95 = (bf16[1,128,3072]{2,1,0:T(8,128)(2,1)}, f32[1,1]{1,0:T(1,128)}) custom-call(bf16[1,128,3072]{2,1,0:T(8,128)(2,1)} %q_hbm.1, bf16[1,128,3072]{2,1,0:T(8,128)(2,1)} %k_hbm.1, bf16[1,128,3072]{2,1,0:T(8,128)(2,1)} %v_hbm.1, bf16[1,128,3072]{2,1,0:T(8,128)(2,1)} %next_hbm.1, s32[1,16]{1,0:T(1,128)} %rest_0_.1, s32[1,64]{1,0:T(1,128)} %rest_1_.1, ...), custom_call_target="tpu_custom_call" | custom-call | tf_op jit(solution)/shard_map/pallas_call | solution.py:420
  58.1 2.1 %copy.12 = bf16[1,128,3072]{2,1,0:T(8,128)(2,1)} copy(bf16[1,128,3072]{2,1,0:T(8,128)(2,1)} %get-tuple-element.8) | data formatting | bytes 1572864
